TPU v7x, 256 devices: a whole 4x4x8 slice. The times are simulated.
256 devices in a mesh: sector: 128 (over z, y_hi, x, core), harm: 2 (over y_lo).
Axes of the slice: x: 4, y: 4 (y_hi: 2, y_lo: 2; y = y_hi * 2 + y_lo), z: 8, core: 2. Of those that a mesh axis runs over, the one named last changes fastest.
Arguments:
- disp: float32 [128, 3, 64, 1024], P('sector', None, 'harm'), may hold values from -0.6 to 0.6
- direction: float32 [128, 3, 64, 1024], P('sector', None, 'harm'), may hold values from -0.6 to 0.6
- stick_state: int32 [128, 128, 1024], P('sector'), may hold values from 0 to 2
- contact_params: float32 [128, 4, 1024], P('sector'), may hold values from 0.3 to 3
- mistuning: float32 [128], replicated, may hold values from 1 to 4
- group_ids: int32 [128], replicated, may hold values from 0 to 31, never falling along the last dimension, each value on 1 to 8 neighbouring positions
- diag_stiff: float32 [64, 128], P('harm'), may hold values from 1 to 10
- cross_stiff: float32 [64, 128], P('harm'), may hold values from -3 to 3
- excitation: float32 [3, 64, 1024, 128], P(None, 'harm', 'sector'), may hold values from -1.8 to 1.8
Outputs:
- residual: float32 [3, 64, 1024, 128], P(None, 'harm', 'sector')
- jvp: float32 [3, 64, 1024, 128], P(None, 'harm', 'sector')
Inputs may be any that keep to these rules, and one draw needn't show every extreme that they name: `group_ids`: the sectors of one group are consecutive and ids never fall; each of the 32 groups holds 1 to 8 sectors.
All inputs are finite; a program needn't handle non-finite values.
Results may differ from a plain program's by a relative error of at most 0.0003.
Values sent between devices are 32-bit elements; how exact they have to be, the bound alone decides.
No kernel may reach another device: no remote copies, remote signals or barrier semaphores. Data moves between devices by JAX's collectives and lax.ppermute only.
A program may use at most 64 MiB of HBM per device.

v0:
```python
import math

import jax
import jax.numpy as jnp
from jax import lax
from jax.sharding import PartitionSpec as P

exact_mode = lax.Precision.HIGHEST


def passed_along(value, axis, steps):
    count = lax.axis_size(axis)
    pairs = [(source, (source + steps) % count) for source in range(count)]
    return lax.ppermute(value, axis, pairs)


def from_behind(block, axis, distance):
    devices = range(lax.axis_size(axis))
    route = [(i - distance, i) for i in devices if i - distance in devices]
    return lax.ppermute(block, axis, route)


def basis_table(coefs, samples):
    coef_index = lax.broadcasted_iota(jnp.int32, (coefs, samples), 0)
    time_index = lax.broadcasted_iota(jnp.int32, (coefs, samples), 1)
    harmonic = coef_index // 2 + 1
    phase = harmonic * time_index % samples
    angle = phase.astype(jnp.float32) * (2.0 * math.pi / samples)
    return jnp.where(coef_index % 2 == 0, jnp.cos(angle), jnp.sin(angle))


def hartley_table(count):
    row_index = lax.broadcasted_iota(jnp.int32, (count, count), 0)
    col_index = lax.broadcasted_iota(jnp.int32, (count, count), 1)
    phase = row_index * col_index % count
    angle = phase.astype(jnp.float32) * (2.0 * math.pi / count)
    return (jnp.cos(angle) + jnp.sin(angle)) / math.sqrt(count)


def contact_law(gaps, dgaps, states_here, params):
    preload = params[0]
    normal_stiff = params[1]
    tangent_stiff = params[2]
    friction_coef = params[3]
    touching = (states_here != 2).astype(jnp.float32)
    sliding = states_here == 1
    normal = (preload + normal_stiff * gaps[0]) * touching
    dnormal = normal_stiff * dgaps[0] * touching
    radius = jnp.sqrt(gaps[1] * gaps[1] + gaps[2] * gaps[2] + 1.0)
    projected = (gaps[1] * dgaps[1] + gaps[2] * dgaps[2]) / (radius * radius * radius)
    tractions = [normal]
    dtractions = [dnormal]
    for channel in (1, 2):
        stuck = tangent_stiff * gaps[channel]
        dstuck = tangent_stiff * dgaps[channel]
        slipped = friction_coef * normal * gaps[channel] / radius
        dslipped = friction_coef * (
            dnormal * gaps[channel] / radius
            + normal * (dgaps[channel] / radius - gaps[channel] * projected)
        )
        tractions.append(jnp.where(sliding, slipped, stuck) * touching)
        dtractions.append(jnp.where(sliding, dslipped, dstuck) * touching)
    return (jnp.stack(tractions), jnp.stack(dtractions))


def mirror(field):
    return jnp.roll(jnp.flip(field, -1), 1, -1)


def group_flag(group_ids, own_group, other_index, sectors):
    inside = jnp.logical_and(other_index >= 0, other_index < sectors)
    safe_index = jnp.clip(other_index, 0, sectors - 1)
    other_group = lax.dynamic_slice_in_dim(group_ids, safe_index, 1)
    return jnp.logical_and(inside, other_group == own_group).astype(jnp.float32)[0]


def body(
    disp,
    direction,
    stick_state,
    contact_params,
    mistuning,
    group_ids,
    diag_stiff,
    cross_stiff,
    excitation,
):
    sectors = lax.axis_size("sector")
    sector_index = lax.axis_index("sector")
    harm_index = lax.axis_index("harm")
    local_coefs = disp.shape[2]
    samples = stick_state.shape[1]
    coefs = local_coefs * lax.axis_size("harm")
    table = basis_table(coefs, samples)
    own_table = lax.dynamic_slice_in_dim(table, harm_index * local_coefs, local_coefs, 0)
    scale = 2.0 / samples
    hartley = hartley_table(sectors)
    paired = jnp.concatenate([disp, direction], 0)
    paired_next = passed_along(paired, "sector", -1)
    relative = paired - paired_next
    gathered = lax.all_gather(relative, "harm", axis=2, tiled=True)
    params_here = contact_params[0]
    gaps = jnp.einsum("wcjp,jt->wctp", gathered, table, precision=exact_mode)
    traction, dtraction = contact_law(gaps[0], gaps[1], stick_state[0], params_here)
    loads = (
        jnp.einsum(
            "wctp,jt->wcjp", jnp.stack([traction, dtraction]), own_table, precision=exact_mode
        )
        * scale
    )
    earlier_loads = passed_along(loads, "sector", 1)
    own_group = lax.dynamic_slice_in_dim(group_ids, sector_index, 1)
    members = jnp.sum((group_ids == own_group[0]).astype(jnp.float32))
    totals = paired
    for offset in range(1, 8):
        from_before = from_behind(paired, "sector", offset)
        from_after = from_behind(paired, "sector", -offset)
        flag_before = group_flag(group_ids, own_group, sector_index - offset, sectors)
        flag_after = group_flag(group_ids, own_group, sector_index + offset, sectors)
        totals = totals + flag_before * from_before + flag_after * from_after
    weight = lax.dynamic_slice_in_dim(mistuning, sector_index, 1)[0]
    forces = loads - earlier_loads + weight * (paired - totals / members)
    outgoing = jnp.concatenate([paired, forces], 0)
    received = lax.all_to_all(outgoing[:, None], "sector", split_axis=4, concat_axis=1, tiled=True)
    states_nd = jnp.einsum("ks,wscjp->wcjpk", hartley, received[0:2], precision=exact_mode)
    forces_nd = jnp.einsum("ks,wscjp->wcjpk", hartley, received[2:4], precision=exact_mode)
    stiff_diag = diag_stiff[None, :, None, :]
    stiff_cross = cross_stiff[None, :, None, :]
    residual = (
        stiff_diag * states_nd[0] + stiff_cross * mirror(states_nd[0]) + forces_nd[0] - excitation
    )
    jvp = stiff_diag * states_nd[1] + stiff_cross * mirror(states_nd[1]) + forces_nd[1]
    return (residual, jvp)


def solution(mesh):
    in_specs = (
        P("sector", None, "harm", None),
        P("sector", None, "harm", None),
        P("sector", None, None),
        P("sector", None, None),
        P(),
        P(),
        P("harm", None),
        P("harm", None),
        P(None, "harm", "sector", None),
    )
    out_specs = (P(None, "harm", "sector", None), P(None, "harm", "sector", None))
    return jax.shard_map(body, mesh=mesh, in_specs=in_specs, out_specs=out_specs, check_vma=False)
```

profile of v0, /device:TPU:1, one launch (start us, length us, event | category | flops | bytes accessed | tf_op | source)
XLA Modules:
  0.0 354.7 jit_solution(15844503535268224859)
XLA Ops:
  7.2 0.0 all-gather.2.cloned.1.call-start
  7.2 1.0 constant_dynamic-update-slice_fusion.1
  8.2 1.0 constant_dynamic-update-slice_fusion
  9.3 0.0 copy-start.10
  9.3 3.3 collective-permute-start
  12.6 9.0 %collective-permute-done = f32[2,3,32,1024]{3,2,1,0:T(8,128)S(1)} collective-permute-done((f32[2,3,32,1024]{3,2,1,0:T(8,128)S(1)}, f32[2,3,32,1024]{3,2,1,0:T(8,128)S(1)}, u32[]{:S(2)}, u32[]{:S(2)}) %collective-permute-start) | collective-permute-done | bytes 786464 | tf_op jit(solution)/shard_map/ppermute | solution.py:14
  21.6 1.0 sub.66
  22.6 0.0 all-gather.2.cloned.1.call-update
  22.7 3.3 collective-permute-start.10
  26.0 1.3 collective-permute-start.11
  27.3 11.4 %collective-permute-start.12 = (f32[2,3,32,1024]{3,2,1,0:T(8,128)S(1)}, f32[2,3,32,1024]{3,2,1,0:T(8,128)}, u32[]{:S(2)}, u32[]{:S(2)}) collective-permute-start(f32[2,3,32,1024]{3,2,1,0:T(8,128)S(1)} %constant_dynamic-update-slice_fusion), channel_id=1, source_target_pairs={{0,12},{2,14},{4,16},{6,18},{8,20},{10,22},{12,24},{14,26},{16,28}... | collective-permute-start | bytes 2359304 | tf_op jit(solution)/shard_map/ppermute | solution.py:20
  38.7 1.3 collective-permute-start.13
  39.9 6.2 %collective-permute-start.14 = (f32[2,3,32,1024]{3,2,1,0:T(8,128)S(1)}, f32[2,3,32,1024]{3,2,1,0:T(8,128)}, u32[]{:S(2)}, u32[]{:S(2)}) collective-permute-start(f32[2,3,32,1024]{3,2,1,0:T(8,128)S(1)} %constant_dynamic-update-slice_fusion), channel_id=1, source_target_pairs={{0,14},{2,16},{4,18},{6,20},{8,22},{10,24},{12,26},{14,28},{16,30}... | collective-permute-start | bytes 2359304 | tf_op jit(solution)/shard_map/ppermute | solution.py:20
  46.2 0.2 sine_select_fusion
  46.4 53.6 %all-gather.2.cloned.1.call-done = f32[2,3,64,1024]{3,2,1,0:T(8,128)} async-done(((f32[2,3,32,1024]{3,2,1,0:T(8,128)}), f32[2,3,64,1024]{3,2,1,0:T(8,128)}) %all-gather.2.cloned.1.call-update) | async-done | bytes 1572880 | tf_op jit(solution)/shard_map/all_gather | solution.py:101
  100.1 4.4 %convolution_bitcast_fusion = f32[2,3,128,1024]{3,2,1,0:T(8,128)S(1)} fusion(f32[2,3,64,1024]{3,2,1,0:T(8,128)} %all-gather.2.cloned.1.call-done, s32[64]{0:T(128)S(1)} %get-tuple-element.34, s32[64]{0:T(128)S(1)} %get-tuple-element.36, s32[64]{0:T(128)S(1)} %get-tuple-element.35, s32[64]{0:T(128)S(1)} %get-tuple-element.37, ...), kind=kOutput, calls=%fused_computation.4 | convolution fusion | flops 604135424 | bytes 4719744 | tf_op jit(solution)/shard_map/wcjp,jt->wctp/dot_general | solution.py:103
  104.5 0.4 select_select_fusion.3
  104.8 0.7 select_select_fusion.1
  105.6 1.3 collective-permute-start.15
  106.9 0.0 collective-permute-done.11
  106.9 33.3 %collective-permute-start.2 = (f32[2,3,32,1024]{3,2,1,0:T(8,128)S(1)}, f32[2,3,32,1024]{3,2,1,0:T(8,128)S(1)}, u32[]{:S(2)}, u32[]{:S(2)}) collective-permute-start(f32[2,3,32,1024]{3,2,1,0:T(8,128)S(1)} %constant_dynamic-update-slice_fusion), channel_id=1, source_target_pairs={{0,2},{2,4},{4,6},{6,8},{8,10},{10,12},{12,14},{14,16},{16,18},{18... | collective-permute-start | bytes 2359304 | tf_op jit(solution)/shard_map/ppermute | solution.py:20
  140.2 1.9 collective-permute-start.3
  142.1 0.0 collective-permute-done.13
  142.2 2.1 collective-permute-start.4
  144.3 1.3 collective-permute-start.5
  145.6 0.1 maximum_bitcast_fusion
  145.7 0.6 select_select_fusion
  146.3 0.2 maximum_bitcast_fusion.1
  146.5 0.0 copy-start.8
  146.5 0.0 copy-start.11
  146.5 1.7 fusion.7
  148.2 7.0 %collective-permute-start.6 = (f32[2,3,32,1024]{3,2,1,0:T(8,128)S(1)}, f32[2,3,32,1024]{3,2,1,0:T(8,128)}, u32[]{:S(2)}, u32[]{:S(2)}) collective-permute-start(f32[2,3,32,1024]{3,2,1,0:T(8,128)S(1)} %constant_dynamic-update-slice_fusion), channel_id=1, source_target_pairs={{0,6},{2,8},{4,10},{6,12},{8,14},{10,16},{12,18},{14,20},{16,22},{... | collective-permute-start | bytes 2359304 | tf_op jit(solution)/shard_map/ppermute | solution.py:20
  155.3 1.3 collective-permute-start.7
  156.6 1.8 collective-permute-done.3
  158.4 9.2 %collective-permute-start.8 = (f32[2,3,32,1024]{3,2,1,0:T(8,128)S(1)}, f32[2,3,32,1024]{3,2,1,0:T(8,128)}, u32[]{:S(2)}, u32[]{:S(2)}) collective-permute-start(f32[2,3,32,1024]{3,2,1,0:T(8,128)S(1)} %constant_dynamic-update-slice_fusion), channel_id=1, source_target_pairs={{0,8},{2,10},{4,12},{6,14},{8,16},{10,18},{12,20},{14,22},{16,24},... | collective-permute-start | bytes 2359304 | tf_op jit(solution)/shard_map/ppermute | solution.py:20
  167.5 5.5 %collective-permute-done.4 = f32[2,3,32,1024]{3,2,1,0:T(8,128)S(1)} collective-permute-done((f32[2,3,32,1024]{3,2,1,0:T(8,128)S(1)}, f32[2,3,32,1024]{3,2,1,0:T(8,128)S(1)}, u32[]{:S(2)}, u32[]{:S(2)}) %collective-permute-start.4) | collective-permute-done | bytes 786464 | tf_op jit(solution)/shard_map/ppermute | solution.py:20
  173.0 1.3 collective-permute-start.9
  174.4 0.9 copy-done.6
  175.2 25.5 %collective-permute-start.1 = (f32[2,3,32,1024]{3,2,1,0:T(8,128)S(1)}, f32[2,3,32,1024]{3,2,1,0:T(8,128)}, u32[]{:S(2)}, u32[]{:S(2)}) collective-permute-start(f32[2,3,32,1024]{3,2,1,0:T(8,128)S(1)} %fusion.7), channel_id=1, source_target_pairs={{0,2},{2,4},{4,6},{6,8},{8,10},{10,12},{12,14},{14,16},{16,18},{18... | collective-permute-start | bytes 2359304 | tf_op jit(solution)/shard_map/ppermute | solution.py:14
  200.7 0.7 fusion.59
  218.9 0.6 dynamic_slice.52
  219.4 1.2 fusion.38
  220.7 4.3 %collective-permute-done.8 = f32[2,3,32,1024]{3,2,1,0:T(8,128)} collective-permute-done((f32[2,3,32,1024]{3,2,1,0:T(8,128)S(1)}, f32[2,3,32,1024]{3,2,1,0:T(8,128)}, u32[]{:S(2)}, u32[]{:S(2)}) %collective-permute-start.8) | collective-permute-done | bytes 786464 | tf_op jit(solution)/shard_map/ppermute | solution.py:20
  225.0 3.6 %collective-permute-done.9 = f32[2,3,32,1024]{3,2,1,0:T(8,128)} collective-permute-done((f32[2,3,32,1024]{3,2,1,0:T(8,128)S(1)}, f32[2,3,32,1024]{3,2,1,0:T(8,128)}, u32[]{:S(2)}, u32[]{:S(2)}) %collective-permute-start.9) | collective-permute-done | bytes 786464 | tf_op jit(solution)/shard_map/ppermute | solution.py:20
  228.6 4.8 %collective-permute-done.1 = f32[2,3,32,1024]{3,2,1,0:T(8,128)} collective-permute-done((f32[2,3,32,1024]{3,2,1,0:T(8,128)S(1)}, f32[2,3,32,1024]{3,2,1,0:T(8,128)}, u32[]{:S(2)}, u32[]{:S(2)}) %collective-permute-start.1) | collective-permute-done | bytes 786464 | tf_op jit(solution)/shard_map/ppermute | solution.py:14
  233.4 6.8 %multiply_add_fusion = f32[2,3,32,1024]{3,2,1,0:T(8,128)S(1)} fusion(f32[2,3,32,1024]{3,2,1,0:T(8,128)S(1)} %constant_dynamic-update-slice_fusion, f32[2,3,32,1024]{3,2,1,0:T(8,128)} %copy-done.2, f32[2,3,32,1024]{3,2,1,0:T(8,128)} %collective-permute-done.14, f32[2,3,32,1024]{3,2,1,0:T(8,128)} %collective-permute-done.13, ...), kind=kLoop, calls=%fused_computation.14 | loop fusion | flops 6488064 | bytes 14155840 | tf_op jit(solution)/shard_map/add | solution.py:122
  240.2 0.1 maximum_bitcast_fusion.2
  240.3 4.6 %copy.17 = f32[4,1,3,32,1024]{3,0,2,1,4:T(4,128)} copy(f32[4,1,3,32,1024]{4,3,2,0,1:T(8,128)S(1)} %maximum_bitcast_fusion.2) | data formatting | bytes 3145728 | tf_op jit(solution)/shard_map/broadcast_in_dim | solution.py:124
  244.9 6.0 %reshape.518 = f32[128,1,3072]{2,1,0:T(1,128)S(1)} reshape(f32[1024,1,3,4,32]{4,3,2,1,0:T(4,128)} %bitcast.140) | data formatting | bytes 3145728
  250.9 76.5 %all_to_all.15 = f32[128,1,3072]{2,1,0:T(1,128)S(1)} all-to-all(f32[128,1,3072]{2,1,0:T(1,128)S(1)} %reshape.518), channel_id=1, replica_groups=mesh['sector'=128,'harm'=2] {'sector'}, dimensions={0} | all-to-all | bytes 3145728 | tf_op jit(solution)/shard_map/all_to_all | solution.py:124
  327.4 0.5 broadcast.307
  328.0 4.4 %reduce = f32[128,3072]{1,0:T(8,128)S(1)} reduce(f32[128,1,3072]{2,1,0:T(1,128)S(1)} %all_to_all.15, f32[]{:T(128)} %broadcast.307), dimensions={1}, to_apply=%all_to_all.11.reduce_sub_computation | reduce | bytes 3145732 | tf_op jit(solution)/shard_map/all_to_all | solution.py:124
  332.3 4.9 %reshape.519 = f32[1024,1,3,4,32]{4,3,2,1,0:T(4,128)} reshape(f32[128,3072]{1,0:T(8,128)S(1)} %reduce) | data formatting | bytes 3145728
  337.3 5.5 %copy.19 = f32[4,1,3,32,128,8]{4,5,3,2,0,1:T(8,128)S(1)} copy(f32[4,1,3,32,128,8]{3,0,2,5,4,1:T(4,128)} %bitcast.141) | data formatting | bytes 3145728 | tf_op jit(solution)/shard_map/all_to_all | solution.py:124
  342.8 1.0 fusion.11
  343.8 1.0 fusion.10
  344.9 0.1 slice_bitcast_fusion.11
  344.9 0.0 copy-start.9
  345.0 0.2 slice.145
  345.1 0.2 slice.127
  345.3 0.2 slice.150
  345.5 0.2 slice.134
  345.6 0.0 copy-done.9
  345.7 2.2 fusion.19
  (30 shorter events, 0.1 us)
Async XLA Ops:
  7.2 92.9 %all-gather.2.cloned.1.call-start = ((), (), s32[]{:S(2)}) async-start(), calls=%async_computation.1 | async-start | bytes 2359296 | tf_op jit(solution)/shard_map/all_gather | solution.py:101
  9.3 36.9 %copy-start.10 = (f32[1,4,1024]{2,1,0:T(4,128)S(1)}, f32[1,4,1024]{2,1,0:T(4,128)}, u32[]{:S(2)}) copy-start(f32[1,4,1024]{2,1,0:T(4,128)} %param.12) | copy-start | bytes 49156
  9.3 12.4 %collective-permute-start = (f32[2,3,32,1024]{3,2,1,0:T(8,128)S(1)}, f32[2,3,32,1024]{3,2,1,0:T(8,128)S(1)}, u32[]{:S(2)}, u32[]{:S(2)}) collective-permute-start(f32[2,3,32,1024]{3,2,1,0:T(8,128)S(1)} %constant_dynamic-update-slice_fusion), channel_id=1, source_target_pairs={{0,254},{2,0},{4,2},{6,4},{8,6},{10,8},{12,10},{14,12},{16,14},{18... | collective-permute-start | bytes 2359304 | tf_op jit(solution)/shard_map/ppermute | solution.py:14
  22.7 82.9 %collective-permute-start.10 = (f32[2,3,32,1024]{3,2,1,0:T(8,128)S(1)}, f32[2,3,32,1024]{3,2,1,0:T(8,128)S(1)}, u32[]{:S(2)}, u32[]{:S(2)}) collective-permute-start(f32[2,3,32,1024]{3,2,1,0:T(8,128)S(1)} %constant_dynamic-update-slice_fusion), channel_id=1, source_target_pairs={{0,10},{2,12},{4,14},{6,16},{8,18},{10,20},{12,22},{14,24},{16,26}... | collective-permute-start | bytes 2359304 | tf_op jit(solution)/shard_map/ppermute | solution.py:20
  26.0 80.9 %collective-permute-start.11 = (f32[2,3,32,1024]{3,2,1,0:T(8,128)S(1)}, f32[2,3,32,1024]{3,2,1,0:T(8,128)S(1)}, u32[]{:S(2)}, u32[]{:S(2)}) collective-permute-start(f32[2,3,32,1024]{3,2,1,0:T(8,128)S(1)} %constant_dynamic-update-slice_fusion), channel_id=1, source_target_pairs={{10,0},{12,2},{14,4},{16,6},{18,8},{20,10},{22,12},{24,14},{26,16}... | collective-permute-start | bytes 2359304 | tf_op jit(solution)/shard_map/ppermute | solution.py:20
  27.3 112.9 %collective-permute-start.12 = (f32[2,3,32,1024]{3,2,1,0:T(8,128)S(1)}, f32[2,3,32,1024]{3,2,1,0:T(8,128)}, u32[]{:S(2)}, u32[]{:S(2)}) collective-permute-start(f32[2,3,32,1024]{3,2,1,0:T(8,128)S(1)} %constant_dynamic-update-slice_fusion), channel_id=1, source_target_pairs={{0,12},{2,14},{4,16},{6,18},{8,20},{10,22},{12,24},{14,26},{16,28}... | collective-permute-start | bytes 2359304 | tf_op jit(solution)/shard_map/ppermute | solution.py:20
  38.7 103.5 %collective-permute-start.13 = (f32[2,3,32,1024]{3,2,1,0:T(8,128)S(1)}, f32[2,3,32,1024]{3,2,1,0:T(8,128)}, u32[]{:S(2)}, u32[]{:S(2)}) collective-permute-start(f32[2,3,32,1024]{3,2,1,0:T(8,128)S(1)} %constant_dynamic-update-slice_fusion), channel_id=1, source_target_pairs={{12,0},{14,2},{16,4},{18,6},{20,8},{22,10},{24,12},{26,14},{28,16}... | collective-permute-start | bytes 2359304 | tf_op jit(solution)/shard_map/ppermute | solution.py:20
  39.9 104.3 %collective-permute-start.14 = (f32[2,3,32,1024]{3,2,1,0:T(8,128)S(1)}, f32[2,3,32,1024]{3,2,1,0:T(8,128)}, u32[]{:S(2)}, u32[]{:S(2)}) collective-permute-start(f32[2,3,32,1024]{3,2,1,0:T(8,128)S(1)} %constant_dynamic-update-slice_fusion), channel_id=1, source_target_pairs={{0,14},{2,16},{4,18},{6,20},{8,22},{10,24},{12,26},{14,28},{16,30}... | collective-permute-start | bytes 2359304 | tf_op jit(solution)/shard_map/ppermute | solution.py:20
  100.1 4.4 %copy-start.7 = (s32[1,128,1024]{2,1,0:T(8,128)S(1)}, s32[1,128,1024]{2,1,0:T(8,128)}, u32[]{:S(2)}) copy-start(s32[1,128,1024]{2,1,0:T(8,128)} %param.11) | copy-start | bytes 1572868
  105.6 42.6 %collective-permute-start.15 = (f32[2,3,32,1024]{3,2,1,0:T(8,128)S(1)}, f32[2,3,32,1024]{3,2,1,0:T(8,128)S(1)}, u32[]{:S(2)}, u32[]{:S(2)}) collective-permute-start(f32[2,3,32,1024]{3,2,1,0:T(8,128)S(1)} %constant_dynamic-update-slice_fusion), channel_id=1, source_target_pairs={{14,0},{16,2},{18,4},{20,6},{22,8},{24,10},{26,12},{28,14},{30,16}... | collective-permute-start | bytes 2359304 | tf_op jit(solution)/shard_map/ppermute | solution.py:20
  106.9 48.4 %collective-permute-start.2 = (f32[2,3,32,1024]{3,2,1,0:T(8,128)S(1)}, f32[2,3,32,1024]{3,2,1,0:T(8,128)S(1)}, u32[]{:S(2)}, u32[]{:S(2)}) collective-permute-start(f32[2,3,32,1024]{3,2,1,0:T(8,128)S(1)} %constant_dynamic-update-slice_fusion), channel_id=1, source_target_pairs={{0,2},{2,4},{4,6},{6,8},{8,10},{10,12},{12,14},{14,16},{16,18},{18... | collective-permute-start | bytes 2359304 | tf_op jit(solution)/shard_map/ppermute | solution.py:20
  140.2 18.2 %collective-permute-start.3 = (f32[2,3,32,1024]{3,2,1,0:T(8,128)S(1)}, f32[2,3,32,1024]{3,2,1,0:T(8,128)S(1)}, u32[]{:S(2)}, u32[]{:S(2)}) collective-permute-start(f32[2,3,32,1024]{3,2,1,0:T(8,128)S(1)} %constant_dynamic-update-slice_fusion), channel_id=1, source_target_pairs={{2,0},{4,2},{6,4},{8,6},{10,8},{12,10},{14,12},{16,14},{18,16},{20... | collective-permute-start | bytes 2359304 | tf_op jit(solution)/shard_map/ppermute | solution.py:20
  142.2 30.9 %collective-permute-start.4 = (f32[2,3,32,1024]{3,2,1,0:T(8,128)S(1)}, f32[2,3,32,1024]{3,2,1,0:T(8,128)S(1)}, u32[]{:S(2)}, u32[]{:S(2)}) collective-permute-start(f32[2,3,32,1024]{3,2,1,0:T(8,128)S(1)} %constant_dynamic-update-slice_fusion), channel_id=1, source_target_pairs={{0,4},{2,6},{4,8},{6,10},{8,12},{10,14},{12,16},{14,18},{16,20},{1... | collective-permute-start | bytes 2359304 | tf_op jit(solution)/shard_map/ppermute | solution.py:20
  144.3 30.0 %collective-permute-start.5 = (f32[2,3,32,1024]{3,2,1,0:T(8,128)S(1)}, f32[2,3,32,1024]{3,2,1,0:T(8,128)S(1)}, u32[]{:S(2)}, u32[]{:S(2)}) collective-permute-start(f32[2,3,32,1024]{3,2,1,0:T(8,128)S(1)} %constant_dynamic-update-slice_fusion), channel_id=1, source_target_pairs={{4,0},{6,2},{8,4},{10,6},{12,8},{14,10},{16,12},{18,14},{20,16},{2... | collective-permute-start | bytes 2359304 | tf_op jit(solution)/shard_map/ppermute | solution.py:20
  146.5 54.2 %copy-start.8 = (s32[128]{0:T(128)S(1)}, s32[128]{0:T(128)}, u32[]{:S(2)}) copy-start(s32[128]{0:T(128)} %param.14) | copy-start | bytes 1540
  146.5 72.4 %copy-start.11 = (f32[128]{0:T(128)S(1)}, f32[128]{0:T(128)}, u32[]{:S(2)}) copy-start(f32[128]{0:T(128)} %param.13) | copy-start | bytes 1540
  148.2 26.1 %copy-start.2 = (f32[2,3,32,1024]{3,2,1,0:T(8,128)}, f32[2,3,32,1024]{3,2,1,0:T(8,128)S(1)}, u32[]{:S(2)}) copy-start(f32[2,3,32,1024]{3,2,1,0:T(8,128)S(1)} %collective-permute-done.15) | copy-start | bytes 2359300
  148.2 72.4 %collective-permute-start.6 = (f32[2,3,32,1024]{3,2,1,0:T(8,128)S(1)}, f32[2,3,32,1024]{3,2,1,0:T(8,128)}, u32[]{:S(2)}, u32[]{:S(2)}) collective-permute-start(f32[2,3,32,1024]{3,2,1,0:T(8,128)S(1)} %constant_dynamic-update-slice_fusion), channel_id=1, source_target_pairs={{0,6},{2,8},{4,10},{6,12},{8,14},{10,16},{12,18},{14,20},{16,22},{... | collective-permute-start | bytes 2359304 | tf_op jit(solution)/shard_map/ppermute | solution.py:20
  155.3 19.1 %copy-start.3 = (f32[2,3,32,1024]{3,2,1,0:T(8,128)}, f32[2,3,32,1024]{3,2,1,0:T(8,128)S(1)}, u32[]{:S(2)}) copy-start(f32[2,3,32,1024]{3,2,1,0:T(8,128)S(1)} %collective-permute-done.2) | copy-start | bytes 2359300
  155.3 65.4 %collective-permute-start.7 = (f32[2,3,32,1024]{3,2,1,0:T(8,128)S(1)}, f32[2,3,32,1024]{3,2,1,0:T(8,128)}, u32[]{:S(2)}, u32[]{:S(2)}) collective-permute-start(f32[2,3,32,1024]{3,2,1,0:T(8,128)S(1)} %constant_dynamic-update-slice_fusion), channel_id=1, source_target_pairs={{6,0},{8,2},{10,4},{12,6},{14,8},{16,10},{18,12},{20,14},{22,16},{... | collective-permute-start | bytes 2359304 | tf_op jit(solution)/shard_map/ppermute | solution.py:20
  158.4 16.0 %copy-start.4 = (f32[2,3,32,1024]{3,2,1,0:T(8,128)}, f32[2,3,32,1024]{3,2,1,0:T(8,128)S(1)}, u32[]{:S(2)}) copy-start(f32[2,3,32,1024]{3,2,1,0:T(8,128)S(1)} %collective-permute-done.3) | copy-start | bytes 2359300
  158.4 66.6 %collective-permute-start.8 = (f32[2,3,32,1024]{3,2,1,0:T(8,128)S(1)}, f32[2,3,32,1024]{3,2,1,0:T(8,128)}, u32[]{:S(2)}, u32[]{:S(2)}) collective-permute-start(f32[2,3,32,1024]{3,2,1,0:T(8,128)S(1)} %constant_dynamic-update-slice_fusion), channel_id=1, source_target_pairs={{0,8},{2,10},{4,12},{6,14},{8,16},{10,18},{12,20},{14,22},{16,24},... | collective-permute-start | bytes 2359304 | tf_op jit(solution)/shard_map/ppermute | solution.py:20
  173.0 1.3 copy-start.5
  173.0 55.6 %collective-permute-start.9 = (f32[2,3,32,1024]{3,2,1,0:T(8,128)S(1)}, f32[2,3,32,1024]{3,2,1,0:T(8,128)}, u32[]{:S(2)}, u32[]{:S(2)}) collective-permute-start(f32[2,3,32,1024]{3,2,1,0:T(8,128)S(1)} %constant_dynamic-update-slice_fusion), channel_id=1, source_target_pairs={{8,0},{10,2},{12,4},{14,6},{16,8},{18,10},{20,12},{22,14},{24,16},... | collective-permute-start | bytes 2359304 | tf_op jit(solution)/shard_map/ppermute | solution.py:20
  174.4 0.9 copy-start.6
  175.2 58.1 %collective-permute-start.1 = (f32[2,3,32,1024]{3,2,1,0:T(8,128)S(1)}, f32[2,3,32,1024]{3,2,1,0:T(8,128)}, u32[]{:S(2)}, u32[]{:S(2)}) collective-permute-start(f32[2,3,32,1024]{3,2,1,0:T(8,128)S(1)} %fusion.7), channel_id=1, source_target_pairs={{0,2},{2,4},{4,6},{6,8},{8,10},{10,12},{12,14},{14,16},{16,18},{18... | collective-permute-start | bytes 2359304 | tf_op jit(solution)/shard_map/ppermute | solution.py:14
  233.4 6.8 %copy-start = (f32[1,3,32,1024]{3,2,1,0:T(8,128)S(1)}, f32[1,3,32,1024]{3,2,1,0:T(8,128)}, u32[]{:S(2)}) copy-start(f32[1,3,32,1024]{3,2,1,0:T(8,128)} %param.9) | copy-start | bytes 1179652
  233.4 6.8 %copy-start.1 = (f32[1,3,32,1024]{3,2,1,0:T(8,128)S(1)}, f32[1,3,32,1024]{3,2,1,0:T(8,128)}, u32[]{:S(2)}) copy-start(f32[1,3,32,1024]{3,2,1,0:T(8,128)} %param.10) | copy-start | bytes 1179652
  344.9 0.7 copy-start.9
Sparse Core Ops, SparseCore 0:
  22.8 77.2 all-gather.1
where the time goes:
time: 357 us; the launch traced here: 355 us
  starting transfers between devices  111 us (31%)
  waiting for transfers between devices  82.7 us (23%)
  blocking collectives  76.5 us (21%)
  between operations  31.9 us (9%)
  local copies, waits for them, and re-layouts  26.5 us (7%)
  other arithmetic  17.9 us (5%)
  matrix products  8.16 us (2%)
    ppermute x14, starting transfers between devices, from_behind(): return lax.ppermute(block, axis, route)  82.1 us
    all_to_all x1, blocking collectives, body(): lax.all_to_all(outgoing[:, None], 'sector', split_axis=4, concat_axis=1,...  76.5 us
    all_gather x1, waiting for transfers between devices, body(): gathered = lax.all_gather(relative, 'harm', axis=2, tiled=True)  53.6 us
    ppermute x2, starting transfers between devices, passed_along(): return lax.ppermute(value, axis, pairs)  28.8 us
    ppermute x14, waiting for transfers between devices, from_behind(): return lax.ppermute(block, axis, route)  15.2 us
    ppermute x2, waiting for transfers between devices, passed_along(): return lax.ppermute(value, axis, pairs)  13.8 us
    unnamed x27, local copies, waits for them, and re-layouts  12.9 us
  transfers between devices with their start and end apart: 17, of which 7 were waited for; matrix products, arithmetic and copies ran while one was open for 3% of the time, Pallas kernels for 0%

commit v1 on v0

v1 whole, which is shorter than its diff:
```python
import math

import jax
import jax.numpy as jnp
import ml_dtypes
import numpy as np
from jax import lax
from jax.experimental import pallas as pl
from jax.experimental.pallas import tpu as pltpu
from jax.sharding import PartitionSpec as P

F32 = jnp.float32
BF16 = jnp.bfloat16
N = 128
HALF = 32
ROWS = 9


def split_np(table):
    hi = table.astype(ml_dtypes.bfloat16)
    lo = (table - hi.astype(np.float64)).astype(ml_dtypes.bfloat16)
    return hi, lo


def tables():
    t = np.arange(N)
    j = np.arange(64) // 2 + 1
    angle = 2 * np.pi * (j[:, None] * t[None, :] % N) / N
    basis = np.where(np.arange(64)[:, None] % 2 == 0, np.cos(angle), np.sin(angle))
    angle = 2 * np.pi * (t[:, None] * t[None, :] % N) / N
    hart = (np.cos(angle) + np.sin(angle)) / math.sqrt(N)
    hart_mirror = (np.cos(angle) - np.sin(angle)) / math.sqrt(N)
    hart_diff = hart - np.roll(hart, -1, axis=0)
    hi, lo = split_np(basis.T)
    to_time = np.concatenate([hi, hi, lo], 1)
    hi, lo = split_np(basis * (2.0 / N))
    to_coef = np.concatenate([hi, hi, lo], 1)
    hi, lo = split_np(hart_diff)
    diff = np.concatenate([hi, hi, lo], 0)
    hi, lo = split_np(np.concatenate([hart, hart_mirror], 1))
    pair = np.concatenate([hi, hi, lo], 0)
    return to_time, to_coef, diff, pair, hart.astype(np.float32)


def halves(x):
    hi = x.astype(BF16)
    lo = (x - hi.astype(F32)).astype(BF16)
    return hi, lo


def mm(a, b):
    return jnp.dot(a, b, preferred_element_type=F32)


def pack_kernel(disp, direction, stick, params, out, scr0, scr1):
    h = lax.axis_index("harm")
    d = disp[0].reshape(96, N)
    e = direction[0].reshape(96, N)
    z = stick[0, pl.ds(pl.multiple_of(h * 64, 64), 64), :].astype(F32)
    scr0[...] = jnp.concatenate([d, e[:32]], 0).T
    scr1[...] = jnp.concatenate([e[32:], z], 0).T
    for i in range(4):
        out[pl.ds(2 * i, 32, stride=ROWS), :] = scr0[pl.ds(i, 32, stride=4), :]
        out[pl.ds(2 * i + 1, 32, stride=ROWS), :] = scr1[pl.ds(i, 32, stride=4), :]
    p = params[0]
    first = jnp.where(h == 0, p[0:1], p[2:3])
    second = pltpu.roll(jnp.where(h == 0, p[1:2], p[3:4]), 4, 1)
    lane = lax.broadcasted_iota(jnp.int32, (32, N), 1) // 4
    row = lax.broadcasted_iota(jnp.int32, (32, N), 0)
    out[pl.ds(8, 32, stride=ROWS), :] = jnp.where(lane == row, first, second)


def pack(disp, direction, stick, params):
    return pl.pallas_call(
        pack_kernel,
        grid=(8,),
        in_specs=[
            pl.BlockSpec((1, 3, 32, N), lambda g: (0, 0, 0, g)),
            pl.BlockSpec((1, 3, 32, N), lambda g: (0, 0, 0, g)),
            pl.BlockSpec((1, 128, N), lambda g: (0, 0, g)),
            pl.BlockSpec((1, 4, N), lambda g: (0, 0, g)),
        ],
        out_specs=pl.BlockSpec((32 * ROWS, N), lambda g: (g, 0)),
        out_shape=jax.ShapeDtypeStruct((256 * ROWS, N), F32),
        scratch_shapes=[pltpu.VMEM((N, N), F32), pltpu.VMEM((N, N), F32)],
        name="pack",
    )(disp, direction, stick, params)


def contact_kernel(
    got, stiff, other_stiff, mist, groups, to_time, to_coef, diff, pair, hart,
    mine, send, wide, tall, res,
):
    i = pl.program_id(0)
    h = lax.axis_index("harm")
    spot = (lax.axis_index("sector") * 2 + h) % 32

    @pl.when(i == 0)
    def _():
        for half in range(2):
            block = got[pl.ds(half * ROWS + 8, N, stride=2 * ROWS), :]
            block = pltpu.roll(block, (N - 4 * spot) % N, 1)
            tall[pl.ds(8 * half, 8), :] = block.T[0:8]
        here = jnp.broadcast_to(groups[...].astype(F32), (N, N))
        same = (here == here.T).astype(F32)
        members = jnp.sum(same, axis=0, keepdims=True)
        row = lax.broadcasted_iota(jnp.int32, (N, N), 0)
        lane = lax.broadcasted_iota(jnp.int32, (N, N), 1)
        pull = ((row == lane).astype(F32) - same / members) * mist[...]
        pulled = jnp.dot(pull, hart[...], preferred_element_type=F32,
                         precision=lax.Precision.HIGHEST)
        hi, lo = halves(pulled)
        wide[:, 0:256] = pair[...]
        wide[:, 256:384] = jnp.concatenate([hi, hi, lo], 0)

    parts = []
    for half in range(2):
        left = got[pl.ds(half * ROWS + 2 * i, N, stride=2 * ROWS), :].T
        right = got[pl.ds(half * ROWS + 2 * i + 1, N, stride=2 * ROWS), :].T
        parts.append((left, right))
    fields = []
    for q in range(6):
        side, at = (0, q) if q < 4 else (1, q - 4)
        fields.append(
            jnp.concatenate([p[side][32 * at : 32 * at + 32] for p in parts], 0)
        )
    state = jnp.concatenate([p[1][64:128] for p in parts], 0)
    x = jnp.concatenate(fields, 1)
    rel = jnp.concatenate([f - pltpu.roll(f, N - 1, 1) for f in fields], 1)
    hi, lo = halves(rel)
    gaps = mm(to_time[...], jnp.concatenate([hi, lo, hi], 0))
    g0, g1, g2, d0, d1, d2 = [gaps[:, N * q : N * q + N] for q in range(6)]
    n0 = tall[pl.ds(i, 1), :]
    kn = tall[pl.ds(4 + i, 1), :]
    kt = tall[pl.ds(8 + i, 1), :]
    mu = tall[pl.ds(12 + i, 1), :]
    touching = state < 1.5
    sliding = jnp.logical_and(state > 0.5, touching)
    sticking = state < 0.5
    normal = n0 + kn * g0
    dnormal = kn * d0
    inv = lax.rsqrt(g1 * g1 + g2 * g2 + 1.0)
    proj = (g1 * d1 + g2 * d2) * (inv * inv)
    u1 = g1 * inv
    u2 = g2 * inv
    force = mu * normal
    dforce = mu * dnormal
    zero = jnp.zeros_like(g0)
    gain = force * inv
    rate = dforce - force * proj
    out = [
        jnp.where(touching, normal, zero),
        jnp.where(sticking, kt * g1, jnp.where(sliding, force * u1, zero)),
        jnp.where(sticking, kt * g2, jnp.where(sliding, force * u2, zero)),
        jnp.where(touching, dnormal, zero),
        jnp.where(sticking, kt * d1, jnp.where(sliding, rate * u1 + gain * d1, zero)),
        jnp.where(sticking, kt * d2, jnp.where(sliding, rate * u2 + gain * d2, zero)),
    ]
    hi, lo = halves(jnp.concatenate(out, 1))
    load = mm(to_coef[...], jnp.concatenate([hi, lo, hi], 0))
    first = jnp.where(h == 0, stiff[...], other_stiff[...])
    second = jnp.where(h == 0, other_stiff[...], stiff[...])
    diag = jnp.concatenate([first[0], second[0]], 0)
    cross = jnp.concatenate([first[1], second[1]], 0)
    for q in range(6):
        hi, lo = halves(x[:, N * q : N * q + N])
        spec = mm(jnp.concatenate([hi, lo, hi], 1), wide[...])
        hi, lo = halves(load[:, N * q : N * q + N])
        total = mm(jnp.concatenate([hi, lo, hi], 1), diff[...])
        res[q] = (
            diag * spec[:, 0:N] + cross * spec[:, N : 2 * N] + spec[:, 2 * N :] + total
        )
    own = pl.multiple_of(h * HALF, HALF)
    other = pl.multiple_of((1 - h) * HALF, HALF)
    mine[...] = res[:, pl.ds(own, HALF), :].reshape(192, N)
    send[...] = res[:, pl.ds(other, HALF), :].reshape(192, N)


def contact(got, stiff, other_stiff, mist, groups):
    consts = tables()
    whole = lambda a: pl.BlockSpec(a.shape, lambda i: (0,) * a.ndim)
    args = (got, stiff, other_stiff, mist, groups) + consts
    return pl.pallas_call(
        contact_kernel,
        grid=(4,),
        in_specs=[whole(a) for a in args],
        out_specs=[pl.BlockSpec((192, N), lambda i: (i, 0))] * 2,
        out_shape=[jax.ShapeDtypeStruct((768, N), F32)] * 2,
        scratch_shapes=[
            pltpu.VMEM((384, 384), BF16),
            pltpu.VMEM((16, N), F32),
            pltpu.VMEM((6, 64, N), F32),
        ],
        name="contact",
    )(*args)


def place_kernel(mine, recv, exc, residual, jvp):
    h = lax.axis_index("harm")
    outs = (residual, jvp)
    for side in range(2):

        @pl.when(h == side)
        def _():
            for source, base in ((mine, 4 * side), (recv, 4 * (1 - side))):
                for w in range(2):
                    for ch in range(3):
                        for i in range(4):
                            rows = pl.ds(ch * 256 + base + i, 32, stride=8)
                            block = source[pl.ds((i * 6 + w * 3 + ch) * 32, 32), :]
                            if w == 0:
                                block = block - exc[rows, :]
                            outs[w][rows, :] = block


def place(mine, recv, exc):
    return pl.pallas_call(
        place_kernel,
        out_shape=[jax.ShapeDtypeStruct((768, N), F32)] * 2,
        name="place",
    )(mine, recv, exc)


def body(
    disp, direction, stick_state, contact_params, mistuning, group_ids,
    diag_stiff, cross_stiff, excitation,
):
    stiff = jnp.stack([diag_stiff, cross_stiff])
    other_stiff = lax.ppermute(stiff, "harm", [(0, 1), (1, 0)])
    packed = pack(disp, direction, stick_state, contact_params)
    got = lax.all_to_all(
        packed.reshape(256, 1, ROWS * N), ("sector", "harm"), 0, 0, tiled=True
    ).reshape(256 * ROWS, N)
    mine, send = contact(
        got, stiff, other_stiff, mistuning.reshape(1, N), group_ids.reshape(1, N)
    )
    recv = lax.ppermute(send, "harm", [(0, 1), (1, 0)])
    residual, jvp = place(mine, recv, excitation.reshape(768, N))
    shape = excitation.shape
    return residual.reshape(shape), jvp.reshape(shape)


def solution(mesh):
    in_specs = (
        P("sector", None, "harm", None),
        P("sector", None, "harm", None),
        P("sector", None, None),
        P("sector", None, None),
        P(),
        P(),
        P("harm", None),
        P("harm", None),
        P(None, "harm", "sector", None),
    )
    out_specs = (P(None, "harm", "sector", None), P(None, "harm", "sector", None))
    return jax.shard_map(body, mesh=mesh, in_specs=in_specs, out_specs=out_specs, check_vma=False)
```

time: 357 us -> 77.9 us (0.22)
  starting transfers between devices: 111 us -> 17.1 us
  blocking collectives: 76.5 us -> 0 us
  waiting for transfers between devices: 82.7 us -> 43 us
  between operations: 31.9 us -> 0.68 us
  local copies, waits for them, and re-layouts: 26.5 us -> 1.77 us
  other arithmetic: 17.9 us -> 0.01 us
  Pallas kernels: 0 us -> 14.8 us
  matrix products: 8.16 us -> 0 us
    ppermute x16 -> x2, starting transfers between devices: 111 us -> 1.48 us  [the longest x1 1.48 us: body(): other_stiff = lax.ppermute(stiff, 'harm', [(0, 1), (1, 0)])]
    all_to_all x1 -> x0, blocking collectives: 76.5 us -> none  [body(): lax.all_to_all(outgoing[:, None], 'sector', split_axis=4, concat_axis=1,...]
    all_gather x1 -> x0, waiting for transfers between devices: 53.6 us -> none  [body(): gathered = lax.all_gather(relative, 'harm', axis=2, tiled=True)]
    all_to_all x0 -> x1, waiting for transfers between devices: none -> 30.8 us  [body(): lax.all_to_all(packed.reshape(256, 1, ROWS * N), ('sector', 'harm'), 0, 0...]
    ppermute x16 -> x2, waiting for transfers between devices: 29.1 us -> 12.2 us  [the longest x1 10.5 us: body(): recv = lax.ppermute(send, 'harm', [(0, 1), (1, 0)])]
    all_to_all x0 -> x1, starting transfers between devices: none -> 15.7 us  [body(): lax.all_to_all(packed.reshape(256, 1, ROWS * N), ('sector', 'harm'), 0, 0...]
    pallas_call x0 -> x3, Pallas kernels: none -> 14.8 us  [the longest x1 6.89 us: contact(): pl.pallas_call(contact_kernel, grid=(4,), in_specs=[whole(a) for a in arg...]
    unnamed x27 -> x12, local copies, waits for them, and re-layouts: 12.9 us -> 1.77 us
  transfers between devices with their start and end apart: 17 -> 3, of which waited for: 7 -> 3; matrix products, arithmetic and copies ran while one was open for 3% -> 0% of each run, Pallas kernels for 0% -> 0%
where the time goes in v1:
time: 77.9 us; the launch traced here: 77.4 us
  waiting for transfers between devices  43 us (55%)
  starting transfers between devices  17.1 us (22%)
  Pallas kernels  14.8 us (19%)
  local copies, waits for them, and re-layouts  1.77 us (2%)
    all_to_all x1, waiting for transfers between devices, body(): lax.all_to_all(packed.reshape(256, 1, ROWS * N), ('sector', 'harm'), 0, 0...  30.8 us
    all_to_all x1, starting transfers between devices, body(): lax.all_to_all(packed.reshape(256, 1, ROWS * N), ('sector', 'harm'), 0, 0...  15.7 us
    ppermute x1, waiting for transfers between devices, body(): recv = lax.ppermute(send, 'harm', [(0, 1), (1, 0)])  10.5 us
    pallas_call x1, Pallas kernels, contact(): pl.pallas_call(contact_kernel, grid=(4,), in_specs=[whole(a) for a in arg...  6.89 us
    pallas_call x1, Pallas kernels, pack(): pl.pallas_call(pack_kernel, grid=(8,), in_specs=[pl.BlockSpec((1, 3, 32,...  5.59 us
    pallas_call x1, Pallas kernels, place(): pl.pallas_call(place_kernel, out_shape=[jax.ShapeDtypeStruct((768, N), F3...  2.29 us
    unnamed x12, local copies, waits for them, and re-layouts  1.77 us
    ppermute x1, waiting for transfers between devices, body(): other_stiff = lax.ppermute(stiff, 'harm', [(0, 1), (1, 0)])  1.67 us
  transfers between devices with their start and end apart: 3, of which 3 were waited for; matrix products, arithmetic and copies ran while one was open for 0% of the time, Pallas kernels for 0%

profile of v1, /device:TPU:1, one launch (start us, length us, event | category | flops | bytes accessed | tf_op | source)
XLA Modules:
  0.0 77.4 jit_solution(11325251384267179254)
XLA Ops:
  0.6 5.6 %pack.1 = f32[2304,128]{1,0:T(8,128)} custom-call(f32[1,3,32,1024]{3,2,1,0:T(8,128)} %disp.1, f32[1,3,32,1024]{3,2,1,0:T(8,128)} %direction.1, s32[1,128,1024]{2,1,0:T(8,128)} %stick.1, f32[1,4,1024]{2,1,0:T(4,128)} %params.1), custom_call_target="tpu_custom_call" | custom-call | tf_op jit(solution)/shard_map/pack/pallas_call | solution.py:74
  6.2 0.0 copy-start.4
  6.2 0.0 copy-start.5
  6.2 15.7 %all-to-all-start = ((f32[256,1,1152]{2,1,0:T(1,128)}), f32[256,1,1152]{2,1,0:T(1,128)S(1)}, u32[]{:S(2)}, u32[]{:S(2)}) async-start(f32[256,1,1152]{2,1,0:T(1,128)} %bitcast.9), calls=%async_computation | async-start | bytes 2359296 | tf_op jit(solution)/shard_map/all_to_all | solution.py:231
  21.9 0.0 copy-done.4
  21.9 0.0 copy-done.5
  21.9 0.0 copy-start.2
  21.9 1.5 %collective-permute-start = (f32[2,32,128]{2,1,0:T(8,128)S(1)}, f32[2,32,128]{2,1,0:T(8,128)S(1)}, u32[]{:S(2)}, u32[]{:S(2)}) collective-permute-start(f32[2,32,128]{2,1,0:T(8,128)S(1)} %pad_maximum_fusion.stiff), channel_id=1, source_target_pairs={{0,1},{1,0},{2,3},{3,2},{4,5},{5,4},{6,7},{7,6},{8,9},{9,8},{10,11... | collective-permute-start | bytes 98312 | tf_op jit(solution)/shard_map/ppermute | solution.py:229
  23.4 1.7 %collective-permute-done.other_stiff = f32[2,32,128]{2,1,0:T(8,128)S(1)} collective-permute-done((f32[2,32,128]{2,1,0:T(8,128)S(1)}, f32[2,32,128]{2,1,0:T(8,128)S(1)}, u32[]{:S(2)}, u32[]{:S(2)}) %collective-permute-start) | collective-permute-done | bytes 32800 | tf_op jit(solution)/shard_map/ppermute | solution.py:229
  25.1 0.0 copy-start.3
  25.1 30.8 %all-to-all-done = f32[256,1,1152]{2,1,0:T(1,128)S(1)} async-done(((f32[256,1,1152]{2,1,0:T(1,128)}), f32[256,1,1152]{2,1,0:T(1,128)S(1)}, u32[]{:S(2)}, u32[]{:S(2)}) %all-to-all-start) | async-done | bytes 1179680 | tf_op jit(solution)/shard_map/all_to_all | solution.py:231
  55.9 0.0 copy-start
  55.9 0.0 copy-done.2
  55.9 0.0 copy-done.3
  55.9 1.0 %copy-done = f32[256,1,1152]{2,1,0:T(1,128)} copy-done((f32[256,1,1152]{2,1,0:T(1,128)}, f32[256,1,1152]{2,1,0:T(1,128)S(1)}, u32[]{:S(2)}) %copy-start) | copy-done | bytes 1179672
  56.9 6.9 %contact.1 = (f32[768,128]{1,0:T(8,128)}, f32[768,128]{1,0:T(8,128)}) custom-call(f32[2304,128]{1,0:T(8,128)} %bitcast.10, f32[2,32,128]{2,1,0:T(8,128)} %copy-done.2, f32[2,32,128]{2,1,0:T(8,128)} %copy-done.3, f32[1,128]{1,0:T(1,128)} %bitcast.14, s32[1,128]{1,0:T(1,128)} %bitcast.15, bf16[128,192]{1,0:T(8,128)(2,1)} %constant.10.clone.to_time, ...), custom_call_target="tpu_custom_call" | custom-call | tf_op jit(solution)/shard_map/contact/pallas_call | solution.py:183
  63.8 0.0 collective-permute-start.1
  63.8 10.5 %collective-permute-done.1.recv = f32[768,128]{1,0:T(8,128)S(1)} collective-permute-done((f32[768,128]{1,0:T(8,128)}, f32[768,128]{1,0:T(8,128)S(1)}, u32[]{:S(2)}, u32[]{:S(2)}) %collective-permute-start.1) | collective-permute-done | bytes 393248 | tf_op jit(solution)/shard_map/ppermute | solution.py:237
  74.3 0.0 copy-start.1
  74.3 0.7 copy-done.1
  75.1 2.3 %place.1 = (f32[768,128]{1,0:T(8,128)}, f32[768,128]{1,0:T(8,128)}) custom-call(f32[768,128]{1,0:T(8,128)} %get-tuple-element.6.mine, f32[768,128]{1,0:T(8,128)} %copy-done.1, f32[768,128]{1,0:T(8,128)} %bitcast.11), custom_call_target="tpu_custom_call" | custom-call | tf_op jit(solution)/shard_map/place/pallas_call | solution.py:217
  (1 shorter events, 0.0 us)
Async XLA Ops:
  6.2 15.7 %copy-start.4 = (f32[32,128]{1,0:T(8,128)S(1)}, f32[32,128]{1,0:T(8,128)}, u32[]{:S(2)}) copy-start(f32[32,128]{1,0:T(8,128)} %param.21) | copy-start | bytes 49156
  6.2 15.7 %copy-start.5 = (f32[32,128]{1,0:T(8,128)S(1)}, f32[32,128]{1,0:T(8,128)}, u32[]{:S(2)}) copy-start(f32[32,128]{1,0:T(8,128)} %param.20) | copy-start | bytes 49156
  6.2 49.7 %all-to-all-start = ((f32[256,1,1152]{2,1,0:T(1,128)}), f32[256,1,1152]{2,1,0:T(1,128)S(1)}, u32[]{:S(2)}, u32[]{:S(2)}) async-start(f32[256,1,1152]{2,1,0:T(1,128)} %bitcast.9), calls=%async_computation | async-start | bytes 2359296 | tf_op jit(solution)/shard_map/all_to_all | solution.py:231
  21.9 34.0 %copy-start.2 = (f32[2,32,128]{2,1,0:T(8,128)}, f32[2,32,128]{2,1,0:T(8,128)S(1)}, u32[]{:S(2)}) copy-start(f32[2,32,128]{2,1,0:T(8,128)S(1)} %pad_maximum_fusion.stiff) | copy-start | bytes 98308
  21.9 3.1 %collective-permute-start = (f32[2,32,128]{2,1,0:T(8,128)S(1)}, f32[2,32,128]{2,1,0:T(8,128)S(1)}, u32[]{:S(2)}, u32[]{:S(2)}) collective-permute-start(f32[2,32,128]{2,1,0:T(8,128)S(1)} %pad_maximum_fusion.stiff), channel_id=1, source_target_pairs={{0,1},{1,0},{2,3},{3,2},{4,5},{5,4},{6,7},{7,6},{8,9},{9,8},{10,11... | collective-permute-start | bytes 98312 | tf_op jit(solution)/shard_map/ppermute | solution.py:229
  25.1 30.8 %copy-start.3 = (f32[2,32,128]{2,1,0:T(8,128)}, f32[2,32,128]{2,1,0:T(8,128)S(1)}, u32[]{:S(2)}) copy-start(f32[2,32,128]{2,1,0:T(8,128)S(1)} %collective-permute-done.other_stiff) | copy-start | bytes 98308
  55.9 1.0 %copy-start = (f32[256,1,1152]{2,1,0:T(1,128)}, f32[256,1,1152]{2,1,0:T(1,128)S(1)}, u32[]{:S(2)}) copy-start(f32[256,1,1152]{2,1,0:T(1,128)S(1)} %all-to-all-done) | copy-start | bytes 3538948
  63.8 10.5 %collective-permute-start.1 = (f32[768,128]{1,0:T(8,128)}, f32[768,128]{1,0:T(8,128)S(1)}, u32[]{:S(2)}, u32[]{:S(2)}) collective-permute-start(f32[768,128]{1,0:T(8,128)} %get-tuple-element.7), channel_id=1, source_target_pairs={{0,1},{1,0},{2,3},{3,2},{4,5},{5,4},{6,7},{7,6},{8,9},{9,8},{10,11... | collective-permute-start | bytes 1179656 | tf_op jit(solution)/shard_map/ppermute | solution.py:237
  74.3 0.7 copy-start.1

commit v2 on v1

v2 whole, which is shorter than its diff:
```python
import functools
import math

import jax
import jax.numpy as jnp
import ml_dtypes
import numpy as np
from jax import lax
from jax.experimental import pallas as pl
from jax.experimental.pallas import tpu as pltpu
from jax.sharding import PartitionSpec as P

F32 = jnp.float32
BF16 = jnp.bfloat16
N = 128
HALF = 32
ROWS = 9


def split_np(table):
    hi = table.astype(ml_dtypes.bfloat16)
    lo = (table - hi.astype(np.float64)).astype(ml_dtypes.bfloat16)
    return hi, lo


def tables():
    t = np.arange(N)
    j = np.arange(64) // 2 + 1
    angle = 2 * np.pi * (j[:, None] * t[None, :] % N) / N
    basis = np.where(np.arange(64)[:, None] % 2 == 0, np.cos(angle), np.sin(angle))
    angle = 2 * np.pi * (t[:, None] * t[None, :] % N) / N
    hart = (np.cos(angle) + np.sin(angle)) / math.sqrt(N)
    hart_mirror = (np.cos(angle) - np.sin(angle)) / math.sqrt(N)
    hart_diff = hart - np.roll(hart, -1, axis=0)
    to_time, to_coef = [], []
    for h in range(2):
        own = np.roll(np.roll(basis, -32 * h, axis=0), -64 * h, axis=1)
        hi, lo = split_np(own.T)
        to_time.append(np.concatenate([hi, hi, lo], 1))
        hi, lo = split_np(own * (2.0 / N))
        to_coef.append(np.concatenate([hi, hi, lo], 1))
    hi, lo = split_np(hart_diff)
    diff = np.concatenate([hi, hi, lo], 0)
    hi, lo = split_np(np.concatenate([hart, hart_mirror], 1))
    pair = np.concatenate([hi, hi, lo], 0)
    return np.stack(to_time), np.stack(to_coef), diff, pair, hart.astype(np.float32)


def halves(x):
    hi = x.astype(BF16)
    lo = (x - hi.astype(F32)).astype(BF16)
    return hi, lo


def mm(a, b):
    return jnp.dot(a, b, preferred_element_type=F32)


def split_rows(x):
    hi, lo = halves(x)
    return jnp.concatenate([hi, lo, hi], 0)


def split_lanes(x):
    hi, lo = halves(x)
    return jnp.concatenate([hi, lo, hi], 1)


VM = pl.BlockSpec(memory_space=pltpu.VMEM)


def limits(megabytes):
    return pltpu.CompilerParams(vmem_limit_bytes=megabytes << 20)


def pack_kernel(disp, direction, stick, params, out, scr0, scr1):
    h = lax.axis_index("harm")
    for k in range(4):
        cols = pl.ds(k * N, N)
        d = disp[0, :, :, cols].reshape(96, N)
        e = direction[0, :, :, cols].reshape(96, N)
        z = stick[0, pl.ds(pl.multiple_of(h * 64, 64), 64), cols].astype(F32)
        scr0[k] = jnp.concatenate([d, e[:32]], 0).T
        scr1[k] = jnp.concatenate([e[32:], z], 0).T
        base = 32 * ROWS * k
        for i in range(4):
            to = pl.ds(base + 2 * i, 32, stride=ROWS)
            out[to, :] = scr0[k, pl.ds(i, 32, stride=4), :]
            to = pl.ds(base + 2 * i + 1, 32, stride=ROWS)
            out[to, :] = scr1[k, pl.ds(i, 32, stride=4), :]
        p = params[0, :, cols]
        first = jnp.where(h == 0, p[0:1], p[2:3])
        second = pltpu.roll(jnp.where(h == 0, p[1:2], p[3:4]), 4, 1)
        lane = lax.broadcasted_iota(jnp.int32, (32, N), 1) // 4
        row = lax.broadcasted_iota(jnp.int32, (32, N), 0)
        out[pl.ds(base + 8, 32, stride=ROWS), :] = jnp.where(lane == row, first, second)


def pack(disp, direction, stick, params):
    return pl.pallas_call(
        pack_kernel,
        grid=(2,),
        in_specs=[
            pl.BlockSpec((1, 3, 32, 4 * N), lambda g: (0, 0, 0, g)),
            pl.BlockSpec((1, 3, 32, 4 * N), lambda g: (0, 0, 0, g)),
            pl.BlockSpec((1, 128, 4 * N), lambda g: (0, 0, g)),
            pl.BlockSpec((1, 4, 4 * N), lambda g: (0, 0, g)),
        ],
        out_specs=pl.BlockSpec((128 * ROWS, N), lambda g: (g, 0)),
        out_shape=jax.ShapeDtypeStruct((256 * ROWS, N), F32),
        scratch_shapes=[pltpu.VMEM((4, N, N), F32), pltpu.VMEM((4, N, N), F32)],
        name="pack",
    )(disp, direction, stick, params)


def prep_kernel(mist, groups, pair, hart, wide):
    here = jnp.broadcast_to(groups[...].astype(F32), (N, N))
    same = (here == here.T).astype(F32)
    members = jnp.sum(same, axis=0, keepdims=True)
    row = lax.broadcasted_iota(jnp.int32, (N, N), 0)
    lane = lax.broadcasted_iota(jnp.int32, (N, N), 1)
    pull = ((row == lane).astype(F32) - same / members) * mist[...]
    pulled = jnp.dot(
        pull, hart[...], preferred_element_type=F32, precision=lax.Precision.HIGHEST
    )
    hi, lo = halves(pulled)
    wide[:, 0:256] = pair[...]
    wide[:, 256:384] = jnp.concatenate([hi, hi, lo], 0)


def prep(mist, groups, pair, hart):
    return pl.pallas_call(
        prep_kernel,
        in_specs=[VM] * 4,
        out_specs=VM,
        out_shape=jax.ShapeDtypeStruct((384, 384), BF16),
        compiler_params=limits(8),
        cost_estimate=pl.CostEstimate(flops=10**8, bytes_accessed=10**6, transcendentals=0),
        name="prep",
    )(mist, groups, pair, hart)


def contact_kernel(w, got, stiff, other, wide, to_time, to_coef, diff, mine, send):
    h = lax.axis_index("harm")
    spot = (lax.axis_index("sector") * 2 + h) % 32
    step = 2 * ROWS
    tall = []
    for half in range(2):
        block = got[pl.ds(half * ROWS + 8, N, stride=step), :]
        block = pltpu.roll(block, (N - 4 * spot) % N, 1).T
        for at in range(2):
            tall.append(
                jnp.concatenate([block[4 * at + i : 4 * at + i + 1] for i in range(4)], 1)
            )
    n0, kn, kt, mu = tall
    disp = [[], [], []]
    dirs = [[], [], []]
    state = []
    for i in range(4):
        parts = []
        for half in (h, 1 - h):
            left = got[pl.ds(half * ROWS + 2 * i, N, stride=step), :].T
            right = got[pl.ds(half * ROWS + 2 * i + 1, N, stride=step), :].T
            parts.append((left, right))
        for q in range(3 + 3 * w):
            side, at = (0, q) if q < 4 else (1, q - 4)
            field = [p[side][32 * at : 32 * at + 32] for p in parts]
            (disp if q < 3 else dirs)[q % 3].append(jnp.concatenate(field, 0))
        state.append(jnp.concatenate([p[1][64:128] for p in parts], 0))
    state = jnp.concatenate(state, 1)
    wave = to_time[h]

    def gap_of(fields):
        rel = [f - pltpu.roll(f, N - 1, 1) for ch in fields for f in ch]
        out = mm(wave, split_rows(jnp.concatenate(rel, 1)))
        return [out[:, 512 * ch : 512 * ch + 512] for ch in range(3)]

    g0, g1, g2 = gap_of(disp)
    touching = state < 1.5
    sticking = state < 0.5
    normal = n0 + kn * g0
    inv = lax.rsqrt(g1 * g1 + g2 * g2 + 1.0)
    zero = jnp.zeros_like(g0)
    gain = mu * normal * inv
    if w == 0:
        coef = jnp.where(sticking, kt, jnp.where(touching, gain, zero))
        out = [jnp.where(touching, normal, zero), coef * g1, coef * g2]
        fields = disp
    else:
        d0, d1, d2 = gap_of(dirs)
        dnormal = kn * d0
        proj = (g1 * d1 + g2 * d2) * (inv * inv)
        rate = mu * dnormal * inv - gain * proj
        coef = jnp.where(sticking, kt, jnp.where(touching, gain, zero))
        rate = jnp.where(sticking, zero, jnp.where(touching, rate, zero))
        out = [
            jnp.where(touching, dnormal, zero),
            coef * d1 + rate * g1,
            coef * d2 + rate * g2,
        ]
        fields = dirs
    load = mm(to_coef[h], split_rows(jnp.concatenate(out, 1)))
    load = jnp.concatenate([load[:, N * q : N * q + N] for q in range(12)], 0)
    x = jnp.concatenate([f for ch in fields for f in ch], 0)
    spec = mm(split_lanes(x), wide[...])
    total = mm(split_lanes(load), diff[...])
    diag = jnp.concatenate([stiff[0], other[0]], 0)
    cross = jnp.concatenate([stiff[1], other[1]], 0)
    for q in range(12):
        rows = slice(64 * q, 64 * q + 64)
        res = (
            diag * spec[rows, 0:N] + cross * spec[rows, N : 2 * N]
            + spec[rows, 2 * N :] + total[rows]
        )
        mine[32 * q : 32 * q + 32, :] = res[0:32]
        send[32 * q : 32 * q + 32, :] = res[32:64]


def contact(w, *args):
    return pl.pallas_call(
        functools.partial(contact_kernel, w),
        in_specs=[VM] * len(args),
        out_specs=[VM] * 2,
        out_shape=[jax.ShapeDtypeStruct((384, N), F32)] * 2,
        compiler_params=limits(32),
        cost_estimate=pl.CostEstimate(flops=10**9, bytes_accessed=4 * 10**6, transcendentals=0),
        name="jvp" if w else "residual",
    )(*args)


def place_kernel(mine, recv, *refs):
    h = lax.axis_index("harm")
    out = refs[-1]
    for side in range(2):

        @pl.when(h == side)
        def _():
            for source, base in ((mine, 4 * side), (recv, 4 * (1 - side))):
                for ch in range(3):
                    for i in range(4):
                        rows = pl.ds(ch * 256 + base + i, 32, stride=8)
                        block = source[pl.ds((ch * 4 + i) * 32, 32), :]
                        if len(refs) == 2:
                            block = block - refs[0][rows, :]
                        out[rows, :] = block


def place(name, *args):
    return pl.pallas_call(
        place_kernel,
        in_specs=[VM] * len(args),
        out_specs=VM,
        out_shape=jax.ShapeDtypeStruct((768, N), F32),
        compiler_params=limits(8),
        cost_estimate=pl.CostEstimate(flops=10**6, bytes_accessed=2 * 10**6, transcendentals=0),
        name=name,
    )(*args)


def swap(x):
    return lax.ppermute(x, "harm", [(0, 1), (1, 0)])


def body(
    disp, direction, stick_state, contact_params, mistuning, group_ids,
    diag_stiff, cross_stiff, excitation,
):
    to_time, to_coef, diff, pair, hart = tables()
    stiff = jnp.stack([diag_stiff, cross_stiff])
    other = swap(stiff)
    packed = pack(disp, direction, stick_state, contact_params)
    got = lax.all_to_all(
        packed.reshape(256, 1, ROWS * N), ("sector", "harm"), 0, 0, tiled=True
    ).reshape(256 * ROWS, N)
    wide = prep(mistuning.reshape(1, N), group_ids.reshape(1, N), pair, hart)
    args = (stiff, other, wide, to_time, to_coef, diff)
    mine0, send0 = contact(0, got, *args)
    send0, got = lax.optimization_barrier((send0, got))
    recv0 = swap(send0)
    mine1, send1 = contact(1, got, *args)
    recv1 = swap(send1)
    shape = excitation.shape
    residual = place("place0", mine0, recv0, excitation.reshape(768, N))
    mine1, residual = lax.optimization_barrier((mine1, residual))
    jvp = place("place1", mine1, recv1)
    return residual.reshape(shape), jvp.reshape(shape)


def solution(mesh):
    in_specs = (
        P("sector", None, "harm", None),
        P("sector", None, "harm", None),
        P("sector", None, None),
        P("sector", None, None),
        P(),
        P(),
        P("harm", None),
        P("harm", None),
        P(None, "harm", "sector", None),
    )
    out_specs = (P(None, "harm", "sector", None), P(None, "harm", "sector", None))
    return jax.shard_map(body, mesh=mesh, in_specs=in_specs, out_specs=out_specs, check_vma=False)
```

time: 77.9 us -> 65.9 us (0.85)
  Pallas kernels: 14.8 us -> 7.95 us
  waiting for transfers between devices: 43 us -> 38.2 us
  local copies, waits for them, and re-layouts: 1.77 us -> 0.06 us
  starting transfers between devices: 17.1 us -> 18.8 us
    pallas_call x3 -> x6, Pallas kernels: 14.8 us -> 7.95 us  [the longest x2 3.41 us: contact(): pl.pallas_call(functools.partial(contact_kernel, w), in_specs=[VM] * len(...]
    ppermute x2 -> x3, waiting for transfers between devices: 12.2 us -> 7.39 us  [swap(): return lax.ppermute(x, 'harm', [(0, 1), (1, 0)])]
    unnamed x12 -> x20, local copies, waits for them, and re-layouts: 1.77 us -> 0.06 us
    ppermute x2 -> x3, starting transfers between devices: 1.48 us -> 3.09 us  [swap(): return lax.ppermute(x, 'harm', [(0, 1), (1, 0)])]
  transfers between devices with their start and end apart: 3 -> 4, of which waited for: 3 -> 4; matrix products, arithmetic and copies ran while one was open for 0% -> 0% of each run, Pallas kernels for 0% -> 5%
where the time goes in v2:
time: 65.9 us; the launch traced here: 65.8 us
  waiting for transfers between devices  38.2 us (58%)
  starting transfers between devices  18.8 us (29%)
  Pallas kernels  7.95 us (12%)
  between operations  0.77 us (1%)
    all_to_all x1, waiting for transfers between devices, body(): lax.all_to_all(packed.reshape(256, 1, ROWS * N), ('sector', 'harm'), 0, 0...  30.9 us
    all_to_all x1, starting transfers between devices, body(): lax.all_to_all(packed.reshape(256, 1, ROWS * N), ('sector', 'harm'), 0, 0...  15.7 us
    ppermute x3, waiting for transfers between devices, swap(): return lax.ppermute(x, 'harm', [(0, 1), (1, 0)])  7.39 us
    pallas_call x2, Pallas kernels, contact(): pl.pallas_call(functools.partial(contact_kernel, w), in_specs=[VM] * len(...  3.41 us
    ppermute x3, starting transfers between devices, swap(): return lax.ppermute(x, 'harm', [(0, 1), (1, 0)])  3.09 us
    pallas_call x1, Pallas kernels, pack(): pl.pallas_call(pack_kernel, grid=(2,), in_specs=[pl.BlockSpec((1, 3, 32,...  2.56 us
    pallas_call x2, Pallas kernels, place(): pl.pallas_call(place_kernel, in_specs=[VM] * len(args), out_specs=VM, out...  1.67 us
  transfers between devices with their start and end apart: 4, of which 4 were waited for; matrix products, arithmetic and copies ran while one was open for 0% of the time, Pallas kernels for 5%

profile of v2, /device:TPU:1, one launch (start us, length us, event | category | flops | bytes accessed | tf_op | source)
XLA Modules:
  0.0 65.8 jit_solution(15985158172410698776)
XLA Ops:
  0.6 2.6 %pack.1 = f32[2304,128]{1,0:T(8,128)} custom-call(f32[1,3,32,1024]{3,2,1,0:T(8,128)} %disp.1, f32[1,3,32,1024]{3,2,1,0:T(8,128)} %direction.1, s32[1,128,1024]{2,1,0:T(8,128)} %stick.1, f32[1,4,1024]{2,1,0:T(4,128)} %params.1), custom_call_target="tpu_custom_call" | custom-call | tf_op jit(solution)/shard_map/pack/pallas_call | solution.py:100
  3.2 0.0 copy-start.8
  3.2 0.0 copy-start.9
  3.2 0.0 copy-start.1
  3.2 0.0 copy-start.2
  3.2 0.0 copy-start.3
  3.2 0.0 copy-start.4
  3.2 0.0 copy-start.5
  3.3 0.0 copy-start.6
  3.3 0.0 copy-start.7
  3.3 15.7 %all-to-all-start = ((f32[256,1,1152]{2,1,0:T(1,128)}), f32[256,1,1152]{2,1,0:T(1,128)S(1)}, u32[]{:S(2)}, u32[]{:S(2)}) async-start(f32[256,1,1152]{2,1,0:T(1,128)} %bitcast.14), calls=%async_computation | async-start | bytes 2359296 | tf_op jit(solution)/shard_map/all_to_all | solution.py:272
  19.0 0.0 copy-done.8
  19.0 0.0 copy-done.9
  19.0 1.5 %collective-permute-start = (f32[2,32,128]{2,1,0:T(8,128)S(1)}, f32[2,32,128]{2,1,0:T(8,128)S(1)}, u32[]{:S(2)}, u32[]{:S(2)}) collective-permute-start(f32[2,32,128]{2,1,0:T(8,128)S(1)} %pad_maximum_fusion.stiff), channel_id=1, source_target_pairs={{0,1},{1,0},{2,3},{3,2},{4,5},{5,4},{6,7},{7,6},{8,9},{9,8},{10,11... | collective-permute-start | bytes 98312 | tf_op jit(solution)/shard_map/ppermute | solution.py:261
  20.5 0.0 copy-done.1
  20.5 0.0 copy-done.2
  20.5 0.0 copy-done.3
  20.5 0.0 copy-done.4
  20.5 0.3 prep.1.wide
  20.8 1.3 %collective-permute-done.other = f32[2,32,128]{2,1,0:T(8,128)S(1)} collective-permute-done((f32[2,32,128]{2,1,0:T(8,128)S(1)}, f32[2,32,128]{2,1,0:T(8,128)S(1)}, u32[]{:S(2)}, u32[]{:S(2)}) %collective-permute-start) | collective-permute-done | bytes 32800 | tf_op jit(solution)/shard_map/ppermute | solution.py:261
  22.1 30.9 %all-to-all-done = f32[256,1,1152]{2,1,0:T(1,128)S(1)} async-done(((f32[256,1,1152]{2,1,0:T(1,128)}), f32[256,1,1152]{2,1,0:T(1,128)S(1)}, u32[]{:S(2)}, u32[]{:S(2)}) %all-to-all-start) | async-done | bytes 1179680 | tf_op jit(solution)/shard_map/all_to_all | solution.py:272
  53.0 0.0 copy-done.5
  53.0 0.0 copy-done.6
  53.0 0.0 copy-done.7
  53.0 1.6 %residual.1 = (f32[384,128]{1,0:T(8,128)S(1)}, f32[384,128]{1,0:T(8,128)S(1)}) custom-call(f32[2304,128]{1,0:T(8,128)S(1)} %bitcast.9, f32[2,32,128]{2,1,0:T(8,128)S(1)} %pad_maximum_fusion.stiff, f32[2,32,128]{2,1,0:T(8,128)S(1)} %collective-permute-done.other, bf16[384,384]{1,0:T(8,128)(2,1)S(1)} %prep.1.wide, bf16[2,128,192]{2,1,0:T(8,128)(2,1)S(1)} %copy-done.5, ...), custom_call_target="tpu_custom_call" | custom-call | flops 1000000000 | bytes 4000000 | tf_op jit(solution)/shard_map/residual/pallas_call | solution.py:220
  54.6 0.0 copy-start
  54.6 0.1 collective-permute-start.1
  54.7 1.8 %jvp.1 = (f32[384,128]{1,0:T(8,128)S(1)}, f32[384,128]{1,0:T(8,128)S(1)}) custom-call(f32[2304,128]{1,0:T(8,128)S(1)} %bitcast.10, f32[2,32,128]{2,1,0:T(8,128)S(1)} %pad_maximum_fusion.stiff, f32[2,32,128]{2,1,0:T(8,128)S(1)} %collective-permute-done.other, bf16[384,384]{1,0:T(8,128)(2,1)S(1)} %prep.1.wide, bf16[2,128,192]{2,1,0:T(8,128)(2,1)S(1)} %copy-done.5, ...), custom_call_target="tpu_custom_call" | custom-call | flops 1000000000 | bytes 4000000 | tf_op jit(solution)/shard_map/jvp/pallas_call | solution.py:220
  56.5 1.5 %collective-permute-start.2 = (f32[384,128]{1,0:T(8,128)S(1)}, f32[384,128]{1,0:T(8,128)S(1)}, u32[]{:S(2)}, u32[]{:S(2)}) collective-permute-start(f32[384,128]{1,0:T(8,128)S(1)} %get-tuple-element.17), channel_id=1, source_target_pairs={{0,1},{1,0},{2,3},{3,2},{4,5},{5,4},{6,7},{7,6},{8,9},{9,8},{10,11... | collective-permute-start | bytes 589832 | tf_op jit(solution)/shard_map/ppermute | solution.py:261
  58.1 2.7 %collective-permute-done.1.recv = f32[384,128]{1,0:T(8,128)S(1)} collective-permute-done((f32[384,128]{1,0:T(8,128)S(1)}, f32[384,128]{1,0:T(8,128)S(1)}, u32[]{:S(2)}, u32[]{:S(2)}) %collective-permute-start.1) | collective-permute-done | bytes 196640 | tf_op jit(solution)/shard_map/ppermute | solution.py:261
  60.8 0.0 copy-done
  60.8 0.9 %place0.1 = f32[768,128]{1,0:T(8,128)} custom-call(f32[384,128]{1,0:T(8,128)S(1)} %get-tuple-element.13.mine, f32[384,128]{1,0:T(8,128)S(1)} %collective-permute-done.1.recv, f32[768,128]{1,0:T(8,128)S(1)} %bitcast.11), custom_call_target="tpu_custom_call" | custom-call | flops 1000000 | bytes 2000000 | tf_op jit(solution)/shard_map/place0/pallas_call | solution.py:249
  61.6 3.4 %collective-permute-done.2.recv = f32[384,128]{1,0:T(8,128)S(1)} collective-permute-done((f32[384,128]{1,0:T(8,128)S(1)}, f32[384,128]{1,0:T(8,128)S(1)}, u32[]{:S(2)}, u32[]{:S(2)}) %collective-permute-start.2) | collective-permute-done | bytes 196640 | tf_op jit(solution)/shard_map/ppermute | solution.py:261
  65.0 0.8 %place1.1 = f32[768,128]{1,0:T(8,128)} custom-call(f32[384,128]{1,0:T(8,128)S(1)} %get-tuple-element.16.mine, f32[384,128]{1,0:T(8,128)S(1)} %collective-permute-done.2.recv), custom_call_target="tpu_custom_call" | custom-call | flops 1000000 | bytes 2000000 | tf_op jit(solution)/shard_map/place1/pallas_call | solution.py:249
  (1 shorter events, 0.0 us)
Async XLA Ops:
  3.2 15.8 %copy-start.8 = (f32[32,128]{1,0:T(8,128)S(1)}, f32[32,128]{1,0:T(8,128)}, u32[]{:S(2)}) copy-start(f32[32,128]{1,0:T(8,128)} %param.21) | copy-start | bytes 49156
  3.2 15.8 %copy-start.9 = (f32[32,128]{1,0:T(8,128)S(1)}, f32[32,128]{1,0:T(8,128)}, u32[]{:S(2)}) copy-start(f32[32,128]{1,0:T(8,128)} %param.20) | copy-start | bytes 49156
  3.2 17.3 %copy-start.1 = (bf16[384,256]{1,0:T(8,128)(2,1)S(1)}, bf16[384,256]{1,0:T(8,128)(2,1)}, u32[]{:S(2)}) copy-start(bf16[384,256]{1,0:T(8,128)(2,1)} %constant.10.clone.pair) | copy-start | bytes 589828
  3.2 17.3 %copy-start.2 = (f32[128,128]{1,0:T(8,128)S(1)}, f32[128,128]{1,0:T(8,128)}, u32[]{:S(2)}) copy-start(f32[128,128]{1,0:T(8,128)} %constant.11.clone.hart) | copy-start | bytes 196612
  3.2 17.3 %copy-start.3 = (f32[128]{0:T(128)S(1)}, f32[128]{0:T(128)}, u32[]{:S(2)}) copy-start(f32[128]{0:T(128)} %param.18) | copy-start | bytes 1540
  3.2 17.2 %copy-start.4 = (s32[128]{0:T(128)S(1)}, s32[128]{0:T(128)}, u32[]{:S(2)}) copy-start(s32[128]{0:T(128)} %param.19) | copy-start | bytes 1540
  3.2 49.7 %copy-start.5 = (bf16[2,128,192]{2,1,0:T(8,128)(2,1)S(1)}, bf16[2,128,192]{2,1,0:T(8,128)(2,1)}, u32[]{:S(2)}) copy-start(bf16[2,128,192]{2,1,0:T(8,128)(2,1)} %constant.12.clone.to_time) | copy-start | bytes 294916
  3.3 49.7 %copy-start.6 = (bf16[2,64,384]{2,1,0:T(8,128)(2,1)S(1)}, bf16[2,64,384]{2,1,0:T(8,128)(2,1)}, u32[]{:S(2)}) copy-start(bf16[2,64,384]{2,1,0:T(8,128)(2,1)} %constant.13.clone.to_coef) | copy-start | bytes 294916
  3.3 49.7 %copy-start.7 = (bf16[384,128]{1,0:T(8,128)(2,1)S(1)}, bf16[384,128]{1,0:T(8,128)(2,1)}, u32[]{:S(2)}) copy-start(bf16[384,128]{1,0:T(8,128)(2,1)} %constant.14.clone.diff) | copy-start | bytes 294916
  3.3 49.7 %all-to-all-start = ((f32[256,1,1152]{2,1,0:T(1,128)}), f32[256,1,1152]{2,1,0:T(1,128)S(1)}, u32[]{:S(2)}, u32[]{:S(2)}) async-start(f32[256,1,1152]{2,1,0:T(1,128)} %bitcast.14), calls=%async_computation | async-start | bytes 2359296 | tf_op jit(solution)/shard_map/all_to_all | solution.py:272
  19.0 3.1 %collective-permute-start = (f32[2,32,128]{2,1,0:T(8,128)S(1)}, f32[2,32,128]{2,1,0:T(8,128)S(1)}, u32[]{:S(2)}, u32[]{:S(2)}) collective-permute-start(f32[2,32,128]{2,1,0:T(8,128)S(1)} %pad_maximum_fusion.stiff), channel_id=1, source_target_pairs={{0,1},{1,0},{2,3},{3,2},{4,5},{5,4},{6,7},{7,6},{8,9},{9,8},{10,11... | collective-permute-start | bytes 98312 | tf_op jit(solution)/shard_map/ppermute | solution.py:261
  54.6 6.2 %copy-start = (f32[3,32,8,128]{3,2,1,0:T(8,128)S(1)}, f32[3,32,8,128]{3,2,1,0:T(8,128)}, u32[]{:S(2)}) copy-start(f32[3,32,8,128]{3,2,1,0:T(8,128)} %param.22) | copy-start | bytes 1179652
  54.6 6.2 %collective-permute-start.1 = (f32[384,128]{1,0:T(8,128)S(1)}, f32[384,128]{1,0:T(8,128)S(1)}, u32[]{:S(2)}, u32[]{:S(2)}) collective-permute-start(f32[384,128]{1,0:T(8,128)S(1)} %get-tuple-element.14), channel_id=1, source_target_pairs={{0,1},{1,0},{2,3},{3,2},{4,5},{5,4},{6,7},{7,6},{8,9},{9,8},{10,11... | collective-permute-start | bytes 589832 | tf_op jit(solution)/shard_map/ppermute | solution.py:261
  56.5 8.4 %collective-permute-start.2 = (f32[384,128]{1,0:T(8,128)S(1)}, f32[384,128]{1,0:T(8,128)S(1)}, u32[]{:S(2)}, u32[]{:S(2)}) collective-permute-start(f32[384,128]{1,0:T(8,128)S(1)} %get-tuple-element.17), channel_id=1, source_target_pairs={{0,1},{1,0},{2,3},{3,2},{4,5},{5,4},{6,7},{7,6},{8,9},{9,8},{10,11... | collective-permute-start | bytes 589832 | tf_op jit(solution)/shard_map/ppermute | solution.py:261

commit v3 on v2

--- a/solution.py
+++ b/solution.py
@@ -140,7 +140,9 @@
     )(mist, groups, pair, hart)
 
 
-def contact_kernel(w, got, stiff, other, wide, to_time, to_coef, diff, mine, send):
+def contact_kernel(
+    fields, part, got, stiff, wide, to_time, to_coef, diff, *outs
+):
     h = lax.axis_index("harm")
     spot = (lax.axis_index("sector") * 2 + h) % 32
     step = 2 * ROWS
@@ -153,78 +155,75 @@
                 jnp.concatenate([block[4 * at + i : 4 * at + i + 1] for i in range(4)], 1)
             )
     n0, kn, kt, mu = tall
-    disp = [[], [], []]
-    dirs = [[], [], []]
-    state = []
+    states = [[[], [], []], [[], [], []]]
+    stick = []
     for i in range(4):
         parts = []
         for half in (h, 1 - h):
             left = got[pl.ds(half * ROWS + 2 * i, N, stride=step), :].T
             right = got[pl.ds(half * ROWS + 2 * i + 1, N, stride=step), :].T
             parts.append((left, right))
-        for q in range(3 + 3 * w):
+        for q in range(3 + 3 * max(fields)):
             side, at = (0, q) if q < 4 else (1, q - 4)
-            field = [p[side][32 * at : 32 * at + 32] for p in parts]
-            (disp if q < 3 else dirs)[q % 3].append(jnp.concatenate(field, 0))
-        state.append(jnp.concatenate([p[1][64:128] for p in parts], 0))
-    state = jnp.concatenate(state, 1)
+            coefs = [p[side][HALF * at : HALF * at + HALF] for p in parts]
+            states[q // 3][q % 3].append(coefs)
+        stick.append(jnp.concatenate([p[1][64:128] for p in parts], 0))
+    stick = jnp.concatenate(stick, 1)
     wave = to_time[h]
 
-    def gap_of(fields):
-        rel = [f - pltpu.roll(f, N - 1, 1) for ch in fields for f in ch]
+    def gap_of(state):
+        all_coefs = [jnp.concatenate(c, 0) for ch in state for c in ch]
+        rel = [f - pltpu.roll(f, N - 1, 1) for f in all_coefs]
         out = mm(wave, split_rows(jnp.concatenate(rel, 1)))
-        return [out[:, 512 * ch : 512 * ch + 512] for ch in range(3)]
-
-    g0, g1, g2 = gap_of(disp)
-    touching = state < 1.5
-    sticking = state < 0.5
+        return jnp.split(out, 3, axis=1)
+
+    g0, g1, g2 = gap_of(states[0])
+    touching = stick < 1.5
+    sticking = stick < 0.5
     normal = n0 + kn * g0
     inv = lax.rsqrt(g1 * g1 + g2 * g2 + 1.0)
     zero = jnp.zeros_like(g0)
     gain = mu * normal * inv
-    if w == 0:
-        coef = jnp.where(sticking, kt, jnp.where(touching, gain, zero))
-        out = [jnp.where(touching, normal, zero), coef * g1, coef * g2]
-        fields = disp
-    else:
-        d0, d1, d2 = gap_of(dirs)
-        dnormal = kn * d0
-        proj = (g1 * d1 + g2 * d2) * (inv * inv)
-        rate = mu * dnormal * inv - gain * proj
-        coef = jnp.where(sticking, kt, jnp.where(touching, gain, zero))
-        rate = jnp.where(sticking, zero, jnp.where(touching, rate, zero))
-        out = [
-            jnp.where(touching, dnormal, zero),
-            coef * d1 + rate * g1,
-            coef * d2 + rate * g2,
-        ]
-        fields = dirs
-    load = mm(to_coef[h], split_rows(jnp.concatenate(out, 1)))
-    load = jnp.concatenate([load[:, N * q : N * q + N] for q in range(12)], 0)
-    x = jnp.concatenate([f for ch in fields for f in ch], 0)
-    spec = mm(split_lanes(x), wide[...])
-    total = mm(split_lanes(load), diff[...])
-    diag = jnp.concatenate([stiff[0], other[0]], 0)
-    cross = jnp.concatenate([stiff[1], other[1]], 0)
-    for q in range(12):
-        rows = slice(64 * q, 64 * q + 64)
-        res = (
-            diag * spec[rows, 0:N] + cross * spec[rows, N : 2 * N]
-            + spec[rows, 2 * N :] + total[rows]
-        )
-        mine[32 * q : 32 * q + 32, :] = res[0:32]
-        send[32 * q : 32 * q + 32, :] = res[32:64]
-
-
-def contact(w, *args):
+    coef = jnp.where(sticking, kt, jnp.where(touching, gain, zero))
+    for w, out in zip(fields, outs):
+        if w == 0:
+            traction = [jnp.where(touching, normal, zero), coef * g1, coef * g2]
+        else:
+            d0, d1, d2 = gap_of(states[1])
+            dnormal = kn * d0
+            proj = (g1 * d1 + g2 * d2) * (inv * inv)
+            rate = mu * dnormal * inv - gain * proj
+            rate = jnp.where(sticking, zero, jnp.where(touching, rate, zero))
+            traction = [
+                jnp.where(touching, dnormal, zero),
+                coef * d1 + rate * g1,
+                coef * d2 + rate * g2,
+            ]
+        weights = to_coef[h, HALF * part : HALF * part + HALF]
+        load = mm(weights, split_rows(jnp.concatenate(traction, 1)))
+        load = jnp.concatenate([load[:, N * q : N * q + N] for q in range(12)], 0)
+        x = jnp.concatenate([c[part] for ch in states[w] for c in ch], 0)
+        spec = mm(split_lanes(x), wide[...])
+        total = mm(split_lanes(load), diff[...])
+        for q in range(12):
+            rows = slice(HALF * q, HALF * q + HALF)
+            out[rows, :] = (
+                stiff[0] * spec[rows, 0:N] + stiff[1] * spec[rows, N : 2 * N]
+                + spec[rows, 2 * N :] + total[rows]
+            )
+
+
+def contact(name, fields, part, *args):
     return pl.pallas_call(
-        functools.partial(contact_kernel, w),
+        functools.partial(contact_kernel, fields, part),
         in_specs=[VM] * len(args),
-        out_specs=[VM] * 2,
-        out_shape=[jax.ShapeDtypeStruct((384, N), F32)] * 2,
+        out_specs=[VM] * len(fields),
+        out_shape=[jax.ShapeDtypeStruct((384, N), F32)] * len(fields),
         compiler_params=limits(32),
-        cost_estimate=pl.CostEstimate(flops=10**9, bytes_accessed=4 * 10**6, transcendentals=0),
-        name="jvp" if w else "residual",
+        cost_estimate=pl.CostEstimate(
+            flops=10**9 * len(fields), bytes_accessed=2 * 10**6, transcendentals=0
+        ),
+        name=name,
     )(*args)
 
 
@@ -273,12 +272,14 @@
         packed.reshape(256, 1, ROWS * N), ("sector", "harm"), 0, 0, tiled=True
     ).reshape(256 * ROWS, N)
     wide = prep(mistuning.reshape(1, N), group_ids.reshape(1, N), pair, hart)
-    args = (stiff, other, wide, to_time, to_coef, diff)
-    mine0, send0 = contact(0, got, *args)
+    args = (wide, to_time, to_coef, diff)
+    (send0,) = contact("send0", (0,), 1, got, other, *args)
     send0, got = lax.optimization_barrier((send0, got))
     recv0 = swap(send0)
-    mine1, send1 = contact(1, got, *args)
+    (send1,) = contact("send1", (1,), 1, got, other, *args)
+    send1, got = lax.optimization_barrier((send1, got))
     recv1 = swap(send1)
+    mine0, mine1 = contact("keep", (0, 1), 0, got, stiff, *args)
     shape = excitation.shape
     residual = place("place0", mine0, recv0, excitation.reshape(768, N))
     mine1, residual = lax.optimization_barrier((mine1, residual))

time: 65.9 us -> 65.6 us (level)
  waiting for transfers between devices: 38.2 us -> 36.4 us
  Pallas kernels: 7.95 us -> 9.5 us
    ppermute x3, waiting for transfers between devices: 7.39 us -> 5.52 us  [swap(): return lax.ppermute(x, 'harm', [(0, 1), (1, 0)])]
    pallas_call x2 -> x3, Pallas kernels: 3.41 us -> 4.97 us  [contact(): pl.pallas_call(functools.partial(contact_kernel, fields, part), in_specs=...]
  transfers between devices with their start and end apart: 4 -> 4, of which waited for: 4 -> 4; matrix products, arithmetic and copies ran while one was open for 0% -> 0% of each run, Pallas kernels for 5% -> 7%
where the time goes in v3:
time: 65.6 us; the launch traced here: 65.5 us
  waiting for transfers between devices  36.4 us (55%)
  starting transfers between devices  18.8 us (29%)
  Pallas kernels  9.5 us (14%)
  between operations  0.77 us (1%)
    all_to_all x1, waiting for transfers between devices, body(): lax.all_to_all(packed.reshape(256, 1, ROWS * N), ('sector', 'harm'), 0, 0...  30.9 us
    all_to_all x1, starting transfers between devices, body(): lax.all_to_all(packed.reshape(256, 1, ROWS * N), ('sector', 'harm'), 0, 0...  15.7 us
    ppermute x3, waiting for transfers between devices, swap(): return lax.ppermute(x, 'harm', [(0, 1), (1, 0)])  5.52 us
    pallas_call x3, Pallas kernels, contact(): pl.pallas_call(functools.partial(contact_kernel, fields, part), in_specs=...  4.97 us
    ppermute x3, starting transfers between devices, swap(): return lax.ppermute(x, 'harm', [(0, 1), (1, 0)])  3.1 us
    pallas_call x1, Pallas kernels, pack(): pl.pallas_call(pack_kernel, grid=(2,), in_specs=[pl.BlockSpec((1, 3, 32,...  2.55 us
    pallas_call x2, Pallas kernels, place(): pl.pallas_call(place_kernel, in_specs=[VM] * len(args), out_specs=VM, out...  1.67 us
  transfers between devices with their start and end apart: 4, of which 4 were waited for; matrix products, arithmetic and copies ran while one was open for 0% of the time, Pallas kernels for 7%

profile of v3, /device:TPU:1, one launch (start us, length us, event | category | flops | bytes accessed | tf_op | source)
XLA Modules:
  0.0 65.5 jit_solution(14670959685846615023)
XLA Ops:
  0.6 2.5 %pack.1 = f32[2304,128]{1,0:T(8,128)} custom-call(f32[1,3,32,1024]{3,2,1,0:T(8,128)} %disp.1, f32[1,3,32,1024]{3,2,1,0:T(8,128)} %direction.1, s32[1,128,1024]{2,1,0:T(8,128)} %stick.1, f32[1,4,1024]{2,1,0:T(4,128)} %params.1), custom_call_target="tpu_custom_call" | custom-call | tf_op jit(solution)/shard_map/pack/pallas_call | solution.py:100
  3.2 0.0 copy-start.8
  3.2 0.0 copy-start.9
  3.2 0.0 copy-start.1
  3.2 0.0 copy-start.2
  3.2 0.0 copy-start.3
  3.2 0.0 copy-start.4
  3.2 0.0 copy-start.5
  3.2 0.0 copy-start.6
  3.3 0.0 copy-start.7
  3.3 15.7 %all-to-all-start = ((f32[256,1,1152]{2,1,0:T(1,128)}), f32[256,1,1152]{2,1,0:T(1,128)S(1)}, u32[]{:S(2)}, u32[]{:S(2)}) async-start(f32[256,1,1152]{2,1,0:T(1,128)} %bitcast.15), calls=%async_computation | async-start | bytes 2359296 | tf_op jit(solution)/shard_map/all_to_all | solution.py:271
  18.9 0.0 copy-done.8
  18.9 0.0 copy-done.9
  19.0 1.5 %collective-permute-start = (f32[2,32,128]{2,1,0:T(8,128)S(1)}, f32[2,32,128]{2,1,0:T(8,128)S(1)}, u32[]{:S(2)}, u32[]{:S(2)}) collective-permute-start(f32[2,32,128]{2,1,0:T(8,128)S(1)} %pad_maximum_fusion.stiff), channel_id=1, source_target_pairs={{0,1},{1,0},{2,3},{3,2},{4,5},{5,4},{6,7},{7,6},{8,9},{9,8},{10,11... | collective-permute-start | bytes 98312 | tf_op jit(solution)/shard_map/ppermute | solution.py:260
  20.4 0.0 copy-done.1
  20.4 0.0 copy-done.2
  20.5 0.0 copy-done.3
  20.5 0.0 copy-done.4
  20.5 0.3 prep.1.wide
  20.8 1.3 %collective-permute-done.stiff = f32[2,32,128]{2,1,0:T(8,128)S(1)} collective-permute-done((f32[2,32,128]{2,1,0:T(8,128)S(1)}, f32[2,32,128]{2,1,0:T(8,128)S(1)}, u32[]{:S(2)}, u32[]{:S(2)}) %collective-permute-start) | collective-permute-done | bytes 32800 | tf_op jit(solution)/shard_map/ppermute | solution.py:260
  22.1 30.9 %all-to-all-done = f32[256,1,1152]{2,1,0:T(1,128)S(1)} async-done(((f32[256,1,1152]{2,1,0:T(1,128)}), f32[256,1,1152]{2,1,0:T(1,128)S(1)}, u32[]{:S(2)}, u32[]{:S(2)}) %all-to-all-start) | async-done | bytes 1179680 | tf_op jit(solution)/shard_map/all_to_all | solution.py:271
  53.0 0.0 copy-done.5
  53.0 0.0 copy-done.6
  53.0 0.0 copy-done.7
  53.0 1.3 %send0.1 = f32[384,128]{1,0:T(8,128)S(1)} custom-call(f32[2304,128]{1,0:T(8,128)S(1)} %bitcast.9, f32[2,32,128]{2,1,0:T(8,128)S(1)} %collective-permute-done.stiff, bf16[384,384]{1,0:T(8,128)(2,1)S(1)} %prep.1.wide, bf16[2,128,192]{2,1,0:T(8,128)(2,1)S(1)} %copy-done.5, bf16[2,64,384]{2,1,0:T(8,128)(2,1)S(1)} %copy-done.6, bf16[384,128]{1,0:T(8,128)(2,1)S(1)} %copy-done.7), custom_call_target="tpu_custom_call" | custom-call | flops 1000000000 | bytes 2000000 | tf_op jit(solution)/shard_map/send0/pallas_call | solution.py:217
  54.3 0.1 collective-permute-start.1
  54.4 1.6 %send1.1 = f32[384,128]{1,0:T(8,128)S(1)} custom-call(f32[2304,128]{1,0:T(8,128)S(1)} %bitcast.10, f32[2,32,128]{2,1,0:T(8,128)S(1)} %collective-permute-done.stiff, bf16[384,384]{1,0:T(8,128)(2,1)S(1)} %prep.1.wide, bf16[2,128,192]{2,1,0:T(8,128)(2,1)S(1)} %copy-done.5, bf16[2,64,384]{2,1,0:T(8,128)(2,1)S(1)} %copy-done.6, bf16[384,128]{1,0:T(8,128)(2,1)S(1)} %copy-done.7), custom_call_target="tpu_custom_call" | custom-call | flops 1000000000 | bytes 2000000 | tf_op jit(solution)/shard_map/send1/pallas_call | solution.py:217
  56.0 0.0 copy-start
  56.0 1.5 %collective-permute-start.2 = (f32[384,128]{1,0:T(8,128)S(1)}, f32[384,128]{1,0:T(8,128)S(1)}, u32[]{:S(2)}, u32[]{:S(2)}) collective-permute-start(f32[384,128]{1,0:T(8,128)S(1)} %send1.1), channel_id=1, source_target_pairs={{0,1},{1,0},{2,3},{3,2},{4,5},{5,4},{6,7},{7,6},{8,9},{9,8},{10,11... | collective-permute-start | bytes 589832 | tf_op jit(solution)/shard_map/ppermute | solution.py:260
  57.5 2.1 %keep.1 = (f32[384,128]{1,0:T(8,128)S(1)}, f32[384,128]{1,0:T(8,128)S(1)}) custom-call(f32[2304,128]{1,0:T(8,128)S(1)} %bitcast.11, f32[2,32,128]{2,1,0:T(8,128)S(1)} %pad_maximum_fusion.stiff, bf16[384,384]{1,0:T(8,128)(2,1)S(1)} %prep.1.wide, bf16[2,128,192]{2,1,0:T(8,128)(2,1)S(1)} %copy-done.5, bf16[2,64,384]{2,1,0:T(8,128)(2,1)S(1)} %copy-done.6, ...), custom_call_target="tpu_custom_call" | custom-call | flops 2000000000 | bytes 2000000 | tf_op jit(solution)/shard_map/keep/pallas_call | solution.py:217
  59.6 0.8 %collective-permute-done.1.recv = f32[384,128]{1,0:T(8,128)S(1)} collective-permute-done((f32[384,128]{1,0:T(8,128)S(1)}, f32[384,128]{1,0:T(8,128)S(1)}, u32[]{:S(2)}, u32[]{:S(2)}) %collective-permute-start.1) | collective-permute-done | bytes 196640 | tf_op jit(solution)/shard_map/ppermute | solution.py:260
  60.5 0.0 copy-done
  60.5 0.9 %place0.1 = f32[768,128]{1,0:T(8,128)} custom-call(f32[384,128]{1,0:T(8,128)S(1)} %get-tuple-element.13.mine, f32[384,128]{1,0:T(8,128)S(1)} %collective-permute-done.1.recv, f32[768,128]{1,0:T(8,128)S(1)} %bitcast.12), custom_call_target="tpu_custom_call" | custom-call | flops 1000000 | bytes 2000000 | tf_op jit(solution)/shard_map/place0/pallas_call | solution.py:248
  61.3 3.4 %collective-permute-done.2.recv = f32[384,128]{1,0:T(8,128)S(1)} collective-permute-done((f32[384,128]{1,0:T(8,128)S(1)}, f32[384,128]{1,0:T(8,128)S(1)}, u32[]{:S(2)}, u32[]{:S(2)}) %collective-permute-start.2) | collective-permute-done | bytes 196640 | tf_op jit(solution)/shard_map/ppermute | solution.py:260
  64.7 0.8 %place1.1 = f32[768,128]{1,0:T(8,128)} custom-call(f32[384,128]{1,0:T(8,128)S(1)} %get-tuple-element.16.mine, f32[384,128]{1,0:T(8,128)S(1)} %collective-permute-done.2.recv), custom_call_target="tpu_custom_call" | custom-call | flops 1000000 | bytes 2000000 | tf_op jit(solution)/shard_map/place1/pallas_call | solution.py:248
  (1 shorter events, 0.0 us)
Async XLA Ops:
  3.2 15.8 %copy-start.8 = (f32[32,128]{1,0:T(8,128)S(1)}, f32[32,128]{1,0:T(8,128)}, u32[]{:S(2)}) copy-start(f32[32,128]{1,0:T(8,128)} %param.21) | copy-start | bytes 49156
  3.2 15.8 %copy-start.9 = (f32[32,128]{1,0:T(8,128)S(1)}, f32[32,128]{1,0:T(8,128)}, u32[]{:S(2)}) copy-start(f32[32,128]{1,0:T(8,128)} %param.20) | copy-start | bytes 49156
  3.2 17.3 %copy-start.1 = (bf16[384,256]{1,0:T(8,128)(2,1)S(1)}, bf16[384,256]{1,0:T(8,128)(2,1)}, u32[]{:S(2)}) copy-start(bf16[384,256]{1,0:T(8,128)(2,1)} %constant.10.clone.pair) | copy-start | bytes 589828
  3.2 17.3 %copy-start.2 = (f32[128,128]{1,0:T(8,128)S(1)}, f32[128,128]{1,0:T(8,128)}, u32[]{:S(2)}) copy-start(f32[128,128]{1,0:T(8,128)} %constant.11.clone.hart) | copy-start | bytes 196612
  3.2 17.3 %copy-start.3 = (f32[128]{0:T(128)S(1)}, f32[128]{0:T(128)}, u32[]{:S(2)}) copy-start(f32[128]{0:T(128)} %param.18) | copy-start | bytes 1540
  3.2 17.2 %copy-start.4 = (s32[128]{0:T(128)S(1)}, s32[128]{0:T(128)}, u32[]{:S(2)}) copy-start(s32[128]{0:T(128)} %param.19) | copy-start | bytes 1540
  3.2 49.7 %copy-start.5 = (bf16[2,128,192]{2,1,0:T(8,128)(2,1)S(1)}, bf16[2,128,192]{2,1,0:T(8,128)(2,1)}, u32[]{:S(2)}) copy-start(bf16[2,128,192]{2,1,0:T(8,128)(2,1)} %constant.12.clone.to_time) | copy-start | bytes 294916
  3.2 49.7 %copy-start.6 = (bf16[2,64,384]{2,1,0:T(8,128)(2,1)S(1)}, bf16[2,64,384]{2,1,0:T(8,128)(2,1)}, u32[]{:S(2)}) copy-start(bf16[2,64,384]{2,1,0:T(8,128)(2,1)} %constant.13.clone.to_coef) | copy-start | bytes 294916
  3.3 49.7 %copy-start.7 = (bf16[384,128]{1,0:T(8,128)(2,1)S(1)}, bf16[384,128]{1,0:T(8,128)(2,1)}, u32[]{:S(2)}) copy-start(bf16[384,128]{1,0:T(8,128)(2,1)} %constant.14.clone.diff) | copy-start | bytes 294916
  3.3 49.7 %all-to-all-start = ((f32[256,1,1152]{2,1,0:T(1,128)}), f32[256,1,1152]{2,1,0:T(1,128)S(1)}, u32[]{:S(2)}, u32[]{:S(2)}) async-start(f32[256,1,1152]{2,1,0:T(1,128)} %bitcast.15), calls=%async_computation | async-start | bytes 2359296 | tf_op jit(solution)/shard_map/all_to_all | solution.py:271
  19.0 3.1 %collective-permute-start = (f32[2,32,128]{2,1,0:T(8,128)S(1)}, f32[2,32,128]{2,1,0:T(8,128)S(1)}, u32[]{:S(2)}, u32[]{:S(2)}) collective-permute-start(f32[2,32,128]{2,1,0:T(8,128)S(1)} %pad_maximum_fusion.stiff), channel_id=1, source_target_pairs={{0,1},{1,0},{2,3},{3,2},{4,5},{5,4},{6,7},{7,6},{8,9},{9,8},{10,11... | collective-permute-start | bytes 98312 | tf_op jit(solution)/shard_map/ppermute | solution.py:260
  54.3 6.2 %collective-permute-start.1 = (f32[384,128]{1,0:T(8,128)S(1)}, f32[384,128]{1,0:T(8,128)S(1)}, u32[]{:S(2)}, u32[]{:S(2)}) collective-permute-start(f32[384,128]{1,0:T(8,128)S(1)} %send0.1), channel_id=1, source_target_pairs={{0,1},{1,0},{2,3},{3,2},{4,5},{5,4},{6,7},{7,6},{8,9},{9,8},{10,11... | collective-permute-start | bytes 589832 | tf_op jit(solution)/shard_map/ppermute | solution.py:260
  56.0 4.5 %copy-start = (f32[3,32,8,128]{3,2,1,0:T(8,128)S(1)}, f32[3,32,8,128]{3,2,1,0:T(8,128)}, u32[]{:S(2)}) copy-start(f32[3,32,8,128]{3,2,1,0:T(8,128)} %param.22) | copy-start | bytes 1179652
  56.0 8.7 %collective-permute-start.2 = (f32[384,128]{1,0:T(8,128)S(1)}, f32[384,128]{1,0:T(8,128)S(1)}, u32[]{:S(2)}, u32[]{:S(2)}) collective-permute-start(f32[384,128]{1,0:T(8,128)S(1)} %send1.1), channel_id=1, source_target_pairs={{0,1},{1,0},{2,3},{3,2},{4,5},{5,4},{6,7},{7,6},{8,9},{9,8},{10,11... | collective-permute-start | bytes 589832 | tf_op jit(solution)/shard_map/ppermute | solution.py:260

commit v4 on v3

--- a/solution.py
+++ b/solution.py
@@ -14,6 +14,8 @@
 BF16 = jnp.bfloat16
 N = 128
 HALF = 32
+PARTS = 2
+WIDE = 1024 // PARTS
 ROWS = 9
 
 
@@ -73,47 +75,32 @@
     return pltpu.CompilerParams(vmem_limit_bytes=megabytes << 20)
 
 
-def pack_kernel(disp, direction, stick, params, out, scr0, scr1):
+def pack_kernel(
+    disp, direction, stick, *refs
+):
+    small_hbm, (packed, wide, vd, ve, vz), refs = refs[:7], refs[7:12], refs[12:]
+    small, (scr0, scr1, turned, sem, small_sem) = refs[:7], refs[7:]
+    params, diag, cross, mist, groups, pair, hart = small
     h = lax.axis_index("harm")
-    for k in range(4):
-        cols = pl.ds(k * N, N)
-        d = disp[0, :, :, cols].reshape(96, N)
-        e = direction[0, :, :, cols].reshape(96, N)
-        z = stick[0, pl.ds(pl.multiple_of(h * 64, 64), 64), cols].astype(F32)
-        scr0[k] = jnp.concatenate([d, e[:32]], 0).T
-        scr1[k] = jnp.concatenate([e[32:], z], 0).T
-        base = 32 * ROWS * k
-        for i in range(4):
-            to = pl.ds(base + 2 * i, 32, stride=ROWS)
-            out[to, :] = scr0[k, pl.ds(i, 32, stride=4), :]
-            to = pl.ds(base + 2 * i + 1, 32, stride=ROWS)
-            out[to, :] = scr1[k, pl.ds(i, 32, stride=4), :]
-        p = params[0, :, cols]
-        first = jnp.where(h == 0, p[0:1], p[2:3])
-        second = pltpu.roll(jnp.where(h == 0, p[1:2], p[3:4]), 4, 1)
-        lane = lax.broadcasted_iota(jnp.int32, (32, N), 1) // 4
-        row = lax.broadcasted_iota(jnp.int32, (32, N), 0)
-        out[pl.ds(base + 8, 32, stride=ROWS), :] = jnp.where(lane == row, first, second)
-
-
-def pack(disp, direction, stick, params):
-    return pl.pallas_call(
-        pack_kernel,
-        grid=(2,),
-        in_specs=[
-            pl.BlockSpec((1, 3, 32, 4 * N), lambda g: (0, 0, 0, g)),
-            pl.BlockSpec((1, 3, 32, 4 * N), lambda g: (0, 0, 0, g)),
-            pl.BlockSpec((1, 128, 4 * N), lambda g: (0, 0, g)),
-            pl.BlockSpec((1, 4, 4 * N), lambda g: (0, 0, g)),
-        ],
-        out_specs=pl.BlockSpec((128 * ROWS, N), lambda g: (g, 0)),
-        out_shape=jax.ShapeDtypeStruct((256 * ROWS, N), F32),
-        scratch_shapes=[pltpu.VMEM((4, N, N), F32), pltpu.VMEM((4, N, N), F32)],
-        name="pack",
-    )(disp, direction, stick, params)
-
-
-def prep_kernel(mist, groups, pair, hart, wide):
+    samples = pl.ds(pl.multiple_of(h * 64, 64), 64)
+    copies, first = [], []
+    for k in (3, 4, 6, 1, 2, 5, 0):
+        first.append(pltpu.make_async_copy(small_hbm[k], small[k], small_sem.at[k]))
+        first[-1].start()
+    for g in range(PARTS):
+        cols = pl.ds(g * WIDE, WIDE)
+        copies.append(
+            [
+                pltpu.make_async_copy(disp.at[0, :, :, cols], vd.at[g], sem.at[g, 0]),
+                pltpu.make_async_copy(direction.at[0, :, :, cols], ve.at[g], sem.at[g, 1]),
+                pltpu.make_async_copy(stick.at[0, samples, cols], vz.at[g], sem.at[g, 2]),
+            ]
+        )
+        for copy in copies[-1]:
+            copy.start()
+
+    for copy in first:
+        copy.wait()
     here = jnp.broadcast_to(groups[...].astype(F32), (N, N))
     same = (here == here.T).astype(F32)
     members = jnp.sum(same, axis=0, keepdims=True)
@@ -127,26 +114,70 @@
     wide[:, 0:256] = pair[...]
     wide[:, 256:384] = jnp.concatenate([hi, hi, lo], 0)
 
-
-def prep(mist, groups, pair, hart):
+    turned[...] = jnp.concatenate([diag[...], cross[...]] * 2, 0).T
+    column = turned[pl.ds(lax.axis_index("sector"), 1), :]
+    column = jnp.broadcast_to(pltpu.roll(column, 8, 1), (32, N))
+    column = pltpu.roll(column, 0, 1, stride=4, stride_axis=0)
+    spot = lax.broadcasted_iota(jnp.int32, (32, N), 0)
+    quad = lax.broadcasted_iota(jnp.int32, (32, N), 1) // 4
+    for k in range(8):
+        g, at = divmod(k * N, WIDE)
+        if at == 0:
+            for copy in copies[g]:
+                copy.wait()
+        cols = pl.ds(at, N)
+        d = vd[g, :, :, cols].reshape(96, N)
+        e = ve[g, :, :, cols].reshape(96, N)
+        z = vz[g, :, cols].astype(F32)
+        scr0[k] = jnp.concatenate([d, e[:32]], 0).T
+        scr1[k] = jnp.concatenate([e[32:], z], 0).T
+        base = 32 * ROWS * k
+        for i in range(4):
+            to = pl.ds(base + 2 * i, 32, stride=ROWS)
+            packed[to, :] = scr0[k, pl.ds(i, 32, stride=4), :]
+            to = pl.ds(base + 2 * i + 1, 32, stride=ROWS)
+            packed[to, :] = scr1[k, pl.ds(i, 32, stride=4), :]
+        p = params[0, :, pl.ds(k * N, N)]
+        near = jnp.where(h == 0, p[0:1], p[2:3])
+        second = pltpu.roll(jnp.where(h == 0, p[1:2], p[3:4]), 4, 1)
+        last = jnp.where(quad == (spot + 1) % 32, second, column)
+        packed[pl.ds(base + 8, 32, stride=ROWS), :] = jnp.where(quad == spot, near, last)
+
+
+def pack(*args):
     return pl.pallas_call(
-        prep_kernel,
-        in_specs=[VM] * 4,
-        out_specs=VM,
-        out_shape=jax.ShapeDtypeStruct((384, 384), BF16),
-        compiler_params=limits(8),
-        cost_estimate=pl.CostEstimate(flops=10**8, bytes_accessed=10**6, transcendentals=0),
-        name="prep",
-    )(mist, groups, pair, hart)
+        pack_kernel,
+        in_specs=[pl.BlockSpec(memory_space=pl.ANY)] * len(args),
+        out_specs=[VM, VM],
+        out_shape=[
+            jax.ShapeDtypeStruct((256 * ROWS, N), F32),
+            jax.ShapeDtypeStruct((384, 384), BF16),
+        ],
+        scratch_shapes=[
+            pltpu.VMEM((PARTS, 3, 32, WIDE), F32),
+            pltpu.VMEM((PARTS, 3, 32, WIDE), F32),
+            pltpu.VMEM((PARTS, 64, WIDE), jnp.int32),
+        ]
+        + [pltpu.VMEM(a.shape, a.dtype) for a in args[3:]]
+        + [
+            pltpu.VMEM((8, N, N), F32),
+            pltpu.VMEM((8, N, N), F32),
+            pltpu.VMEM((N, N), F32),
+            pltpu.SemaphoreType.DMA((PARTS, 3)),
+            pltpu.SemaphoreType.DMA((7,)),
+        ],
+        compiler_params=limits(40),
+        name="pack",
+    )(*[pltpu.with_memory_space_constraint(a, pltpu.HBM) for a in args])
 
 
 def contact_kernel(
-    fields, part, got, stiff, wide, to_time, to_coef, diff, *outs
+    fields, part, got, wide, to_time, to_coef, diff, *outs
 ):
     h = lax.axis_index("harm")
     spot = (lax.axis_index("sector") * 2 + h) % 32
     step = 2 * ROWS
-    tall = []
+    tall, stiff = [], []
     for half in range(2):
         block = got[pl.ds(half * ROWS + 8, N, stride=step), :]
         block = pltpu.roll(block, (N - 4 * spot) % N, 1).T
@@ -154,6 +185,9 @@
             tall.append(
                 jnp.concatenate([block[4 * at + i : 4 * at + i + 1] for i in range(4)], 1)
             )
+        stiff.append(block[8:72])
+    stiff = jnp.where(h == part, stiff[0], stiff[1])
+    diag, cross = stiff[0:HALF], stiff[HALF:64]
     n0, kn, kt, mu = tall
     states = [[[], [], []], [[], [], []]]
     stick = []
@@ -208,7 +242,7 @@
         for q in range(12):
             rows = slice(HALF * q, HALF * q + HALF)
             out[rows, :] = (
-                stiff[0] * spec[rows, 0:N] + stiff[1] * spec[rows, N : 2 * N]
+                diag * spec[rows, 0:N] + cross * spec[rows, N : 2 * N]
                 + spec[rows, 2 * N :] + total[rows]
             )
 
@@ -265,21 +299,21 @@
     diag_stiff, cross_stiff, excitation,
 ):
     to_time, to_coef, diff, pair, hart = tables()
-    stiff = jnp.stack([diag_stiff, cross_stiff])
-    other = swap(stiff)
-    packed = pack(disp, direction, stick_state, contact_params)
+    packed, wide = pack(
+        disp, direction, stick_state, contact_params, diag_stiff, cross_stiff,
+        mistuning.reshape(1, N), group_ids.reshape(1, N), jnp.asarray(pair), jnp.asarray(hart),
+    )
     got = lax.all_to_all(
         packed.reshape(256, 1, ROWS * N), ("sector", "harm"), 0, 0, tiled=True
     ).reshape(256 * ROWS, N)
-    wide = prep(mistuning.reshape(1, N), group_ids.reshape(1, N), pair, hart)
     args = (wide, to_time, to_coef, diff)
-    (send0,) = contact("send0", (0,), 1, got, other, *args)
+    (send0,) = contact("send0", (0,), 1, got, *args)
     send0, got = lax.optimization_barrier((send0, got))
     recv0 = swap(send0)
-    (send1,) = contact("send1", (1,), 1, got, other, *args)
+    (send1,) = contact("send1", (1,), 1, got, *args)
     send1, got = lax.optimization_barrier((send1, got))
     recv1 = swap(send1)
-    mine0, mine1 = contact("keep", (0, 1), 0, got, stiff, *args)
+    mine0, mine1 = contact("keep", (0, 1), 0, got, *args)
     shape = excitation.shape
     residual = place("place0", mine0, recv0, excitation.reshape(768, N))
     mine1, residual = lax.optimization_barrier((mine1, residual))

time: 65.6 us -> 65.1 us (level)
  blocking collectives: 0 us -> 49.5 us
  waiting for transfers between devices: 36.4 us -> 4.17 us
  starting transfers between devices: 18.8 us -> 1.62 us
    all_to_all x0 -> x1, blocking collectives: none -> 49.5 us  [body(): lax.all_to_all(packed.reshape(256, 1, ROWS * N), ('sector', 'harm'), 0, 0...]
    all_to_all x1 -> x0, waiting for transfers between devices: 30.9 us -> none  [body(): lax.all_to_all(packed.reshape(256, 1, ROWS * N), ('sector', 'harm'), 0, 0...]
    all_to_all x1 -> x0, starting transfers between devices: 15.7 us -> none  [body(): lax.all_to_all(packed.reshape(256, 1, ROWS * N), ('sector', 'harm'), 0, 0...]
    ppermute x3 -> x2, starting transfers between devices: 3.1 us -> 1.62 us  [swap(): return lax.ppermute(x, 'harm', [(0, 1), (1, 0)])]
    ppermute x3 -> x2, waiting for transfers between devices: 5.52 us -> 4.17 us  [swap(): return lax.ppermute(x, 'harm', [(0, 1), (1, 0)])]
    pallas_call x2 -> x1, Pallas kernels: 2.86 us -> 2.32 us  [pack(): pl.pallas_call(pack_kernel, in_specs=[pl.BlockSpec(memory_space=pl.ANY)]...]
  transfers between devices with their start and end apart: 4 -> 2, of which waited for: 4 -> 2; matrix products, arithmetic and copies ran while one was open for 0% -> 0% of each run, Pallas kernels for 7% -> 7%
where the time goes in v4:
time: 65.1 us; the launch traced here: 65 us
  blocking collectives  49.5 us (76%)
  Pallas kernels  8.97 us (14%)
  waiting for transfers between devices  4.17 us (6%)
  starting transfers between devices  1.62 us (2%)
  between operations  0.71 us (1%)
    all_to_all x1, blocking collectives, body(): lax.all_to_all(packed.reshape(256, 1, ROWS * N), ('sector', 'harm'), 0, 0...  49.5 us
    pallas_call x3, Pallas kernels, contact(): pl.pallas_call(functools.partial(contact_kernel, fields, part), in_specs=...  4.98 us
    ppermute x2, waiting for transfers between devices, swap(): return lax.ppermute(x, 'harm', [(0, 1), (1, 0)])  4.17 us
    pallas_call x1, Pallas kernels, pack(): pl.pallas_call(pack_kernel, in_specs=[pl.BlockSpec(memory_space=pl.ANY)]...  2.32 us
    pallas_call x2, Pallas kernels, place(): pl.pallas_call(place_kernel, in_specs=[VM] * len(args), out_specs=VM, out...  1.67 us
    ppermute x2, starting transfers between devices, swap(): return lax.ppermute(x, 'harm', [(0, 1), (1, 0)])  1.62 us
  transfers between devices with their start and end apart: 2, of which 2 were waited for; matrix products, arithmetic and copies ran while one was open for 0% of the time, Pallas kernels for 7%

profile of v4, /device:TPU:1, one launch (start us, length us, event | category | flops | bytes accessed | tf_op | source)
XLA Modules:
  0.0 65.0 jit_solution(11488094256628407007)
XLA Ops:
  0.6 2.3 %pack.1 = (f32[2304,128]{1,0:T(8,128)S(1)}, bf16[384,384]{1,0:T(8,128)(2,1)S(1)}) custom-call(f32[1,3,32,1024]{3,2,1,0:T(8,128)} %disp.1, f32[1,3,32,1024]{3,2,1,0:T(8,128)} %direction.1, s32[1,128,1024]{2,1,0:T(8,128)} %stick.1, f32[1,4,1024]{2,1,0:T(4,128)} %refs_0_.1, f32[32,128]{1,0:T(8,128)} %refs_1_.1, f32[32,128]{1,0:T(8,128)} %refs_2_.1, ...), custom_call_target="tpu_custom_call" | custom-call | tf_op jit(solution)/shard_map/pack/pallas_call | solution.py:148
  3.0 0.0 copy-start.1
  3.0 0.0 copy-start.2
  3.0 0.0 copy-start.3
  3.0 49.5 %all_to_all.5 = f32[256,1,1152]{2,1,0:T(1,128)S(1)} all-to-all(f32[256,1,1152]{2,1,0:T(1,128)S(1)} %bitcast.10), channel_id=1, replica_groups=mesh['sector'=128,'harm'=2] {'sector','harm'}, dimensions={0} | all-to-all | bytes 2359296 | tf_op jit(solution)/shard_map/all_to_all | solution.py:306
  52.5 0.0 copy-done.1
  52.5 0.0 copy-done.2
  52.5 0.0 copy-done.3
  52.5 1.3 %send0.1 = f32[384,128]{1,0:T(8,128)S(1)} custom-call(f32[2304,128]{1,0:T(8,128)S(1)} %bitcast.7, bf16[384,384]{1,0:T(8,128)(2,1)S(1)} %get-tuple-element.13.wide, bf16[2,128,192]{2,1,0:T(8,128)(2,1)S(1)} %copy-done.1, bf16[2,64,384]{2,1,0:T(8,128)(2,1)S(1)} %copy-done.3, bf16[384,128]{1,0:T(8,128)(2,1)S(1)} %copy-done.2), custom_call_target="tpu_custom_call" | custom-call | flops 1000000000 | bytes 2000000 | tf_op jit(solution)/shard_map/send0/pallas_call | solution.py:251
  53.8 0.1 collective-permute-start
  53.9 1.6 %send1.1 = f32[384,128]{1,0:T(8,128)S(1)} custom-call(f32[2304,128]{1,0:T(8,128)S(1)} %bitcast.8, bf16[384,384]{1,0:T(8,128)(2,1)S(1)} %get-tuple-element.13.wide, bf16[2,128,192]{2,1,0:T(8,128)(2,1)S(1)} %copy-done.1, bf16[2,64,384]{2,1,0:T(8,128)(2,1)S(1)} %copy-done.3, bf16[384,128]{1,0:T(8,128)(2,1)S(1)} %copy-done.2), custom_call_target="tpu_custom_call" | custom-call | flops 1000000000 | bytes 2000000 | tf_op jit(solution)/shard_map/send1/pallas_call | solution.py:251
  55.5 0.0 copy-start
  55.5 1.5 %collective-permute-start.1 = (f32[384,128]{1,0:T(8,128)S(1)}, f32[384,128]{1,0:T(8,128)S(1)}, u32[]{:S(2)}, u32[]{:S(2)}) collective-permute-start(f32[384,128]{1,0:T(8,128)S(1)} %send1.1), channel_id=1, source_target_pairs={{0,1},{1,0},{2,3},{3,2},{4,5},{5,4},{6,7},{7,6},{8,9},{9,8},{10,11... | collective-permute-start | bytes 589832 | tf_op jit(solution)/shard_map/ppermute | solution.py:294
  57.0 2.1 %keep.1 = (f32[384,128]{1,0:T(8,128)S(1)}, f32[384,128]{1,0:T(8,128)S(1)}) custom-call(f32[2304,128]{1,0:T(8,128)S(1)} %bitcast.9, bf16[384,384]{1,0:T(8,128)(2,1)S(1)} %get-tuple-element.13.wide, bf16[2,128,192]{2,1,0:T(8,128)(2,1)S(1)} %copy-done.1, bf16[2,64,384]{2,1,0:T(8,128)(2,1)S(1)} %copy-done.3, bf16[384,128]{1,0:T(8,128)(2,1)S(1)} %copy-done.2), custom_call_target="tpu_custom_call" | custom-call | flops 2000000000 | bytes 2000000 | tf_op jit(solution)/shard_map/keep/pallas_call | solution.py:251
  59.1 0.8 %collective-permute-done.recv = f32[384,128]{1,0:T(8,128)S(1)} collective-permute-done((f32[384,128]{1,0:T(8,128)S(1)}, f32[384,128]{1,0:T(8,128)S(1)}, u32[]{:S(2)}, u32[]{:S(2)}) %collective-permute-start) | collective-permute-done | bytes 196640 | tf_op jit(solution)/shard_map/ppermute | solution.py:294
  60.0 0.0 copy-done
  60.0 0.9 %place0.1 = f32[768,128]{1,0:T(8,128)} custom-call(f32[384,128]{1,0:T(8,128)S(1)} %get-tuple-element.17.mine, f32[384,128]{1,0:T(8,128)S(1)} %collective-permute-done.recv, f32[768,128]{1,0:T(8,128)S(1)} %bitcast.11), custom_call_target="tpu_custom_call" | custom-call | flops 1000000 | bytes 2000000 | tf_op jit(solution)/shard_map/place0/pallas_call | solution.py:282
  60.8 3.4 %collective-permute-done.1.recv = f32[384,128]{1,0:T(8,128)S(1)} collective-permute-done((f32[384,128]{1,0:T(8,128)S(1)}, f32[384,128]{1,0:T(8,128)S(1)}, u32[]{:S(2)}, u32[]{:S(2)}) %collective-permute-start.1) | collective-permute-done | bytes 196640 | tf_op jit(solution)/shard_map/ppermute | solution.py:294
  64.2 0.8 %place1.1 = f32[768,128]{1,0:T(8,128)} custom-call(f32[384,128]{1,0:T(8,128)S(1)} %get-tuple-element.20.mine, f32[384,128]{1,0:T(8,128)S(1)} %collective-permute-done.1.recv), custom_call_target="tpu_custom_call" | custom-call | flops 1000000 | bytes 2000000 | tf_op jit(solution)/shard_map/place1/pallas_call | solution.py:282
Async XLA Ops:
  3.0 49.5 %copy-start.1 = (bf16[2,128,192]{2,1,0:T(8,128)(2,1)S(1)}, bf16[2,128,192]{2,1,0:T(8,128)(2,1)}, u32[]{:S(2)}) copy-start(bf16[2,128,192]{2,1,0:T(8,128)(2,1)} %constant.12.clone.to_time) | copy-start | bytes 294916
  3.0 49.5 %copy-start.2 = (bf16[384,128]{1,0:T(8,128)(2,1)S(1)}, bf16[384,128]{1,0:T(8,128)(2,1)}, u32[]{:S(2)}) copy-start(bf16[384,128]{1,0:T(8,128)(2,1)} %constant.14.clone.diff) | copy-start | bytes 294916
  3.0 49.5 %copy-start.3 = (bf16[2,64,384]{2,1,0:T(8,128)(2,1)S(1)}, bf16[2,64,384]{2,1,0:T(8,128)(2,1)}, u32[]{:S(2)}) copy-start(bf16[2,64,384]{2,1,0:T(8,128)(2,1)} %constant.13.clone.to_coef) | copy-start | bytes 294916
  53.8 6.2 %collective-permute-start = (f32[384,128]{1,0:T(8,128)S(1)}, f32[384,128]{1,0:T(8,128)S(1)}, u32[]{:S(2)}, u32[]{:S(2)}) collective-permute-start(f32[384,128]{1,0:T(8,128)S(1)} %send0.1), channel_id=1, source_target_pairs={{0,1},{1,0},{2,3},{3,2},{4,5},{5,4},{6,7},{7,6},{8,9},{9,8},{10,11... | collective-permute-start | bytes 589832 | tf_op jit(solution)/shard_map/ppermute | solution.py:294
  55.5 4.5 %copy-start = (f32[3,32,8,128]{3,2,1,0:T(8,128)S(1)}, f32[3,32,8,128]{3,2,1,0:T(8,128)}, u32[]{:S(2)}) copy-start(f32[3,32,8,128]{3,2,1,0:T(8,128)} %param.22) | copy-start | bytes 1179652
  55.5 8.7 %collective-permute-start.1 = (f32[384,128]{1,0:T(8,128)S(1)}, f32[384,128]{1,0:T(8,128)S(1)}, u32[]{:S(2)}, u32[]{:S(2)}) collective-permute-start(f32[384,128]{1,0:T(8,128)S(1)} %send1.1), channel_id=1, source_target_pairs={{0,1},{1,0},{2,3},{3,2},{4,5},{5,4},{6,7},{7,6},{8,9},{9,8},{10,11... | collective-permute-start | bytes 589832 | tf_op jit(solution)/shard_map/ppermute | solution.py:294

commit v5 on v4

--- a/solution.py
+++ b/solution.py
@@ -14,8 +14,6 @@
 BF16 = jnp.bfloat16
 N = 128
 HALF = 32
-PARTS = 2
-WIDE = 1024 // PARTS
 ROWS = 9
 
 
@@ -78,27 +76,21 @@
 def pack_kernel(
     disp, direction, stick, *refs
 ):
-    small_hbm, (packed, wide, vd, ve, vz), refs = refs[:7], refs[7:12], refs[12:]
-    small, (scr0, scr1, turned, sem, small_sem) = refs[:7], refs[7:]
-    params, diag, cross, mist, groups, pair, hart = small
+    small_hbm, (packed, pull_hat, vd, ve, vz), refs = refs[:6], refs[6:11], refs[11:]
+    small, (scr0, scr1, turned, sem, small_sem) = refs[:6], refs[6:]
+    params, diag, cross, mist, groups, hart = small
     h = lax.axis_index("harm")
     samples = pl.ds(pl.multiple_of(h * 64, 64), 64)
-    copies, first = [], []
-    for k in (3, 4, 6, 1, 2, 5, 0):
-        first.append(pltpu.make_async_copy(small_hbm[k], small[k], small_sem.at[k]))
-        first[-1].start()
-    for g in range(PARTS):
-        cols = pl.ds(g * WIDE, WIDE)
-        copies.append(
-            [
-                pltpu.make_async_copy(disp.at[0, :, :, cols], vd.at[g], sem.at[g, 0]),
-                pltpu.make_async_copy(direction.at[0, :, :, cols], ve.at[g], sem.at[g, 1]),
-                pltpu.make_async_copy(stick.at[0, samples, cols], vz.at[g], sem.at[g, 2]),
-            ]
-        )
-        for copy in copies[-1]:
-            copy.start()
-
+    first = [
+        pltpu.make_async_copy(small_hbm[k], small[k], small_sem.at[k]) for k in range(6)
+    ]
+    copies = []
+    for ch in range(3):
+        copies.append(pltpu.make_async_copy(disp.at[0, ch], vd.at[ch], sem.at[ch]))
+        copies.append(pltpu.make_async_copy(direction.at[0, ch], ve.at[ch], sem.at[3 + ch]))
+    copies.append(pltpu.make_async_copy(stick.at[0, samples], vz, sem.at[6]))
+    for copy in first + copies:
+        copy.start()
     for copy in first:
         copy.wait()
     here = jnp.broadcast_to(groups[...].astype(F32), (N, N))
@@ -111,8 +103,7 @@
         pull, hart[...], preferred_element_type=F32, precision=lax.Precision.HIGHEST
     )
     hi, lo = halves(pulled)
-    wide[:, 0:256] = pair[...]
-    wide[:, 256:384] = jnp.concatenate([hi, hi, lo], 0)
+    pull_hat[...] = jnp.concatenate([hi, hi, lo], 0)
 
     turned[...] = jnp.concatenate([diag[...], cross[...]] * 2, 0).T
     column = turned[pl.ds(lax.axis_index("sector"), 1), :]
@@ -120,15 +111,13 @@
     column = pltpu.roll(column, 0, 1, stride=4, stride_axis=0)
     spot = lax.broadcasted_iota(jnp.int32, (32, N), 0)
     quad = lax.broadcasted_iota(jnp.int32, (32, N), 1) // 4
+    for copy in copies:
+        copy.wait()
     for k in range(8):
-        g, at = divmod(k * N, WIDE)
-        if at == 0:
-            for copy in copies[g]:
-                copy.wait()
-        cols = pl.ds(at, N)
-        d = vd[g, :, :, cols].reshape(96, N)
-        e = ve[g, :, :, cols].reshape(96, N)
-        z = vz[g, :, cols].astype(F32)
+        cols = pl.ds(k * N, N)
+        d = vd[:, :, cols].reshape(96, N)
+        e = ve[:, :, cols].reshape(96, N)
+        z = vz[:, cols].astype(F32)
         scr0[k] = jnp.concatenate([d, e[:32]], 0).T
         scr1[k] = jnp.concatenate([e[32:], z], 0).T
         base = 32 * ROWS * k
@@ -151,20 +140,20 @@
         out_specs=[VM, VM],
         out_shape=[
             jax.ShapeDtypeStruct((256 * ROWS, N), F32),
-            jax.ShapeDtypeStruct((384, 384), BF16),
+            jax.ShapeDtypeStruct((384, N), BF16),
         ],
         scratch_shapes=[
-            pltpu.VMEM((PARTS, 3, 32, WIDE), F32),
-            pltpu.VMEM((PARTS, 3, 32, WIDE), F32),
-            pltpu.VMEM((PARTS, 64, WIDE), jnp.int32),
+            pltpu.VMEM((3, 32, 8 * N), F32),
+            pltpu.VMEM((3, 32, 8 * N), F32),
+            pltpu.VMEM((64, 8 * N), jnp.int32),
         ]
         + [pltpu.VMEM(a.shape, a.dtype) for a in args[3:]]
         + [
             pltpu.VMEM((8, N, N), F32),
             pltpu.VMEM((8, N, N), F32),
             pltpu.VMEM((N, N), F32),
-            pltpu.SemaphoreType.DMA((PARTS, 3)),
             pltpu.SemaphoreType.DMA((7,)),
+            pltpu.SemaphoreType.DMA((6,)),
         ],
         compiler_params=limits(40),
         name="pack",
@@ -172,7 +161,7 @@
 
 
 def contact_kernel(
-    fields, part, got, wide, to_time, to_coef, diff, *outs
+    fields, part, got, pair, pull_hat, to_time, to_coef, diff, *outs
 ):
     h = lax.axis_index("harm")
     spot = (lax.axis_index("sector") * 2 + h) % 32
@@ -237,13 +226,13 @@
         load = mm(weights, split_rows(jnp.concatenate(traction, 1)))
         load = jnp.concatenate([load[:, N * q : N * q + N] for q in range(12)], 0)
         x = jnp.concatenate([c[part] for ch in states[w] for c in ch], 0)
-        spec = mm(split_lanes(x), wide[...])
-        total = mm(split_lanes(load), diff[...])
+        x = split_lanes(x)
+        spec = mm(x, pair[...])
+        total = mm(x, pull_hat[...]) + mm(split_lanes(load), diff[...])
         for q in range(12):
             rows = slice(HALF * q, HALF * q + HALF)
             out[rows, :] = (
-                diag * spec[rows, 0:N] + cross * spec[rows, N : 2 * N]
-                + spec[rows, 2 * N :] + total[rows]
+                diag * spec[rows, 0:N] + cross * spec[rows, N : 2 * N] + total[rows]
             )
 
 
@@ -299,14 +288,14 @@
     diag_stiff, cross_stiff, excitation,
 ):
     to_time, to_coef, diff, pair, hart = tables()
-    packed, wide = pack(
+    packed, pull_hat = pack(
         disp, direction, stick_state, contact_params, diag_stiff, cross_stiff,
-        mistuning.reshape(1, N), group_ids.reshape(1, N), jnp.asarray(pair), jnp.asarray(hart),
+        mistuning.reshape(1, N), group_ids.reshape(1, N), jnp.asarray(hart),
     )
     got = lax.all_to_all(
         packed.reshape(256, 1, ROWS * N), ("sector", "harm"), 0, 0, tiled=True
     ).reshape(256 * ROWS, N)
-    args = (wide, to_time, to_coef, diff)
+    args = (pair, pull_hat, to_time, to_coef, diff)
     (send0,) = contact("send0", (0,), 1, got, *args)
     send0, got = lax.optimization_barrier((send0, got))
     recv0 = swap(send0)

time: 65.1 us -> 64.8 us (level)
  no operation moved by 1% of the time
where the time goes in v5:
time: 64.8 us; the launch traced here: 64.7 us
  blocking collectives  49.5 us (76%)
  Pallas kernels  8.41 us (13%)
  waiting for transfers between devices  4.42 us (7%)
  starting transfers between devices  1.61 us (2%)
  between operations  0.71 us (1%)
    all_to_all x1, blocking collectives, body(): lax.all_to_all(packed.reshape(256, 1, ROWS * N), ('sector', 'harm'), 0, 0...  49.5 us
    pallas_call x3, Pallas kernels, contact(): pl.pallas_call(functools.partial(contact_kernel, fields, part), in_specs=...  4.64 us
    ppermute x2, waiting for transfers between devices, swap(): return lax.ppermute(x, 'harm', [(0, 1), (1, 0)])  4.42 us
    pallas_call x1, Pallas kernels, pack(): pl.pallas_call(pack_kernel, in_specs=[pl.BlockSpec(memory_space=pl.ANY)]...  2.1 us
    pallas_call x2, Pallas kernels, place(): pl.pallas_call(place_kernel, in_specs=[VM] * len(args), out_specs=VM, out...  1.67 us
    ppermute x2, starting transfers between devices, swap(): return lax.ppermute(x, 'harm', [(0, 1), (1, 0)])  1.61 us
  transfers between devices with their start and end apart: 2, of which 2 were waited for; matrix products, arithmetic and copies ran while one was open for 0% of the time, Pallas kernels for 7%

profile of v5, /device:TPU:1, one launch (start us, length us, event | category | flops | bytes accessed | tf_op | source)
XLA Modules:
  0.0 64.7 jit_solution(8877371412829158763)
XLA Ops:
  0.6 2.1 %pack.1 = (f32[2304,128]{1,0:T(8,128)S(1)}, bf16[384,128]{1,0:T(8,128)(2,1)S(1)}) custom-call(f32[1,3,32,1024]{3,2,1,0:T(8,128)} %disp.1, f32[1,3,32,1024]{3,2,1,0:T(8,128)} %direction.1, s32[1,128,1024]{2,1,0:T(8,128)} %stick.1, f32[1,4,1024]{2,1,0:T(4,128)} %refs_0_.1, f32[32,128]{1,0:T(8,128)} %refs_1_.1, f32[32,128]{1,0:T(8,128)} %refs_2_.1, ...), custom_call_target="tpu_custom_call" | custom-call | tf_op jit(solution)/shard_map/pack/pallas_call | solution.py:137
  2.7 0.0 copy-start.1
  2.8 0.0 copy-start.2
  2.8 0.0 copy-start.3
  2.8 0.0 copy-start.4
  2.8 49.5 %all_to_all.5 = f32[256,1,1152]{2,1,0:T(1,128)S(1)} all-to-all(f32[256,1,1152]{2,1,0:T(1,128)S(1)} %bitcast.10), channel_id=1, replica_groups=mesh['sector'=128,'harm'=2] {'sector','harm'}, dimensions={0} | all-to-all | bytes 2359296 | tf_op jit(solution)/shard_map/all_to_all | solution.py:295
  52.3 0.0 copy-done.1
  52.3 0.0 copy-done.2
  52.3 0.0 copy-done.3
  52.3 0.0 copy-done.4
  52.3 1.2 %send0.1 = f32[384,128]{1,0:T(8,128)S(1)} custom-call(f32[2304,128]{1,0:T(8,128)S(1)} %bitcast.7, bf16[384,256]{1,0:T(8,128)(2,1)S(1)} %copy-done.1, bf16[384,128]{1,0:T(8,128)(2,1)S(1)} %get-tuple-element.13.pull_hat, bf16[2,128,192]{2,1,0:T(8,128)(2,1)S(1)} %copy-done.2, bf16[2,64,384]{2,1,0:T(8,128)(2,1)S(1)} %copy-done.4, bf16[384,128]{1,0:T(8,128)(2,1)S(1)} %copy-done.3), custom_call_target="tpu_custom_call" | custom-call | flops 1000000000 | bytes 2000000 | tf_op jit(solution)/shard_map/send0/pallas_call | solution.py:240
  53.5 0.1 collective-permute-start
  53.6 1.6 %send1.1 = f32[384,128]{1,0:T(8,128)S(1)} custom-call(f32[2304,128]{1,0:T(8,128)S(1)} %bitcast.8, bf16[384,256]{1,0:T(8,128)(2,1)S(1)} %copy-done.1, bf16[384,128]{1,0:T(8,128)(2,1)S(1)} %get-tuple-element.13.pull_hat, bf16[2,128,192]{2,1,0:T(8,128)(2,1)S(1)} %copy-done.2, bf16[2,64,384]{2,1,0:T(8,128)(2,1)S(1)} %copy-done.4, bf16[384,128]{1,0:T(8,128)(2,1)S(1)} %copy-done.3), custom_call_target="tpu_custom_call" | custom-call | flops 1000000000 | bytes 2000000 | tf_op jit(solution)/shard_map/send1/pallas_call | solution.py:240
  55.1 0.0 copy-start
  55.2 1.5 %collective-permute-start.1 = (f32[384,128]{1,0:T(8,128)S(1)}, f32[384,128]{1,0:T(8,128)S(1)}, u32[]{:S(2)}, u32[]{:S(2)}) collective-permute-start(f32[384,128]{1,0:T(8,128)S(1)} %send1.1), channel_id=1, source_target_pairs={{0,1},{1,0},{2,3},{3,2},{4,5},{5,4},{6,7},{7,6},{8,9},{9,8},{10,11... | collective-permute-start | bytes 589832 | tf_op jit(solution)/shard_map/ppermute | solution.py:283
  56.7 1.9 %keep.1 = (f32[384,128]{1,0:T(8,128)S(1)}, f32[384,128]{1,0:T(8,128)S(1)}) custom-call(f32[2304,128]{1,0:T(8,128)S(1)} %bitcast.9, bf16[384,256]{1,0:T(8,128)(2,1)S(1)} %copy-done.1, bf16[384,128]{1,0:T(8,128)(2,1)S(1)} %get-tuple-element.13.pull_hat, bf16[2,128,192]{2,1,0:T(8,128)(2,1)S(1)} %copy-done.2, bf16[2,64,384]{2,1,0:T(8,128)(2,1)S(1)} %copy-done.4, ...), custom_call_target="tpu_custom_call" | custom-call | flops 2000000000 | bytes 2000000 | tf_op jit(solution)/shard_map/keep/pallas_call | solution.py:240
  58.6 1.1 %collective-permute-done.recv = f32[384,128]{1,0:T(8,128)S(1)} collective-permute-done((f32[384,128]{1,0:T(8,128)S(1)}, f32[384,128]{1,0:T(8,128)S(1)}, u32[]{:S(2)}, u32[]{:S(2)}) %collective-permute-start) | collective-permute-done | bytes 196640 | tf_op jit(solution)/shard_map/ppermute | solution.py:283
  59.7 0.0 copy-done
  59.7 0.9 %place0.1 = f32[768,128]{1,0:T(8,128)} custom-call(f32[384,128]{1,0:T(8,128)S(1)} %get-tuple-element.17.mine, f32[384,128]{1,0:T(8,128)S(1)} %collective-permute-done.recv, f32[768,128]{1,0:T(8,128)S(1)} %bitcast.11), custom_call_target="tpu_custom_call" | custom-call | flops 1000000 | bytes 2000000 | tf_op jit(solution)/shard_map/place0/pallas_call | solution.py:271
  60.5 3.4 %collective-permute-done.1.recv = f32[384,128]{1,0:T(8,128)S(1)} collective-permute-done((f32[384,128]{1,0:T(8,128)S(1)}, f32[384,128]{1,0:T(8,128)S(1)}, u32[]{:S(2)}, u32[]{:S(2)}) %collective-permute-start.1) | collective-permute-done | bytes 196640 | tf_op jit(solution)/shard_map/ppermute | solution.py:283
  63.9 0.8 %place1.1 = f32[768,128]{1,0:T(8,128)} custom-call(f32[384,128]{1,0:T(8,128)S(1)} %get-tuple-element.20.mine, f32[384,128]{1,0:T(8,128)S(1)} %collective-permute-done.1.recv), custom_call_target="tpu_custom_call" | custom-call | flops 1000000 | bytes 2000000 | tf_op jit(solution)/shard_map/place1/pallas_call | solution.py:271
Async XLA Ops:
  2.7 49.6 %copy-start.1 = (bf16[384,256]{1,0:T(8,128)(2,1)S(1)}, bf16[384,256]{1,0:T(8,128)(2,1)}, u32[]{:S(2)}) copy-start(bf16[384,256]{1,0:T(8,128)(2,1)} %constant.11.clone.pair) | copy-start | bytes 589828
  2.8 49.5 %copy-start.2 = (bf16[2,128,192]{2,1,0:T(8,128)(2,1)S(1)}, bf16[2,128,192]{2,1,0:T(8,128)(2,1)}, u32[]{:S(2)}) copy-start(bf16[2,128,192]{2,1,0:T(8,128)(2,1)} %constant.12.clone.to_time) | copy-start | bytes 294916
  2.8 49.5 %copy-start.3 = (bf16[384,128]{1,0:T(8,128)(2,1)S(1)}, bf16[384,128]{1,0:T(8,128)(2,1)}, u32[]{:S(2)}) copy-start(bf16[384,128]{1,0:T(8,128)(2,1)} %constant.14.clone.diff) | copy-start | bytes 294916
  2.8 49.5 %copy-start.4 = (bf16[2,64,384]{2,1,0:T(8,128)(2,1)S(1)}, bf16[2,64,384]{2,1,0:T(8,128)(2,1)}, u32[]{:S(2)}) copy-start(bf16[2,64,384]{2,1,0:T(8,128)(2,1)} %constant.13.clone.to_coef) | copy-start | bytes 294916
  53.5 6.2 %collective-permute-start = (f32[384,128]{1,0:T(8,128)S(1)}, f32[384,128]{1,0:T(8,128)S(1)}, u32[]{:S(2)}, u32[]{:S(2)}) collective-permute-start(f32[384,128]{1,0:T(8,128)S(1)} %send0.1), channel_id=1, source_target_pairs={{0,1},{1,0},{2,3},{3,2},{4,5},{5,4},{6,7},{7,6},{8,9},{9,8},{10,11... | collective-permute-start | bytes 589832 | tf_op jit(solution)/shard_map/ppermute | solution.py:283
  55.1 4.5 %copy-start = (f32[3,32,8,128]{3,2,1,0:T(8,128)S(1)}, f32[3,32,8,128]{3,2,1,0:T(8,128)}, u32[]{:S(2)}) copy-start(f32[3,32,8,128]{3,2,1,0:T(8,128)} %param.22) | copy-start | bytes 1179652
  55.2 8.7 %collective-permute-start.1 = (f32[384,128]{1,0:T(8,128)S(1)}, f32[384,128]{1,0:T(8,128)S(1)}, u32[]{:S(2)}, u32[]{:S(2)}) collective-permute-start(f32[384,128]{1,0:T(8,128)S(1)} %send1.1), channel_id=1, source_target_pairs={{0,1},{1,0},{2,3},{3,2},{4,5},{5,4},{6,7},{7,6},{8,9},{9,8},{10,11... | collective-permute-start | bytes 589832 | tf_op jit(solution)/shard_map/ppermute | solution.py:283

commit v6 on v5

--- a/solution.py
+++ b/solution.py
@@ -252,27 +252,35 @@
 
 def place_kernel(mine, recv, *refs):
     h = lax.axis_index("harm")
-    out = refs[-1]
-    for side in range(2):
-
-        @pl.when(h == side)
-        def _():
-            for source, base in ((mine, 4 * side), (recv, 4 * (1 - side))):
-                for ch in range(3):
+    out, whole, sem = refs[-3:]
+    leave = []
+    for ch in range(3):
+        for side in range(2):
+
+            @pl.when(h == side)
+            def _():
+                for source, base in ((mine, 4 * side), (recv, 4 * (1 - side))):
                     for i in range(4):
                         rows = pl.ds(ch * 256 + base + i, 32, stride=8)
                         block = source[pl.ds((ch * 4 + i) * 32, 32), :]
-                        if len(refs) == 2:
+                        if len(refs) == 4:
                             block = block - refs[0][rows, :]
-                        out[rows, :] = block
+                        whole[rows, :] = block
+
+        span = pl.ds(ch * 256, 256)
+        leave.append(pltpu.make_async_copy(whole.at[span], out.at[span], sem.at[ch]))
+        leave[-1].start()
+    for copy in leave:
+        copy.wait()
 
 
 def place(name, *args):
     return pl.pallas_call(
         place_kernel,
         in_specs=[VM] * len(args),
-        out_specs=VM,
+        out_specs=pl.BlockSpec(memory_space=pltpu.HBM),
         out_shape=jax.ShapeDtypeStruct((768, N), F32),
+        scratch_shapes=[pltpu.VMEM((768, N), F32), pltpu.SemaphoreType.DMA((3,))],
         compiler_params=limits(8),
         cost_estimate=pl.CostEstimate(flops=10**6, bytes_accessed=2 * 10**6, transcendentals=0),
         name=name,

time: 64.8 us -> 64.8 us (level)
  no operation moved by 1% of the time
where the time goes in v6:
time: 64.8 us; the launch traced here: 64.7 us
  blocking collectives  49.5 us (76%)
  Pallas kernels  8.33 us (13%)
  waiting for transfers between devices  4.46 us (7%)
  starting transfers between devices  1.61 us (2%)
  between operations  0.72 us (1%)
    all_to_all x1, blocking collectives, body(): lax.all_to_all(packed.reshape(256, 1, ROWS * N), ('sector', 'harm'), 0, 0...  49.5 us
    pallas_call x3, Pallas kernels, contact(): pl.pallas_call(functools.partial(contact_kernel, fields, part), in_specs=...  4.64 us
    ppermute x2, waiting for transfers between devices, swap(): return lax.ppermute(x, 'harm', [(0, 1), (1, 0)])  4.46 us
    pallas_call x1, Pallas kernels, pack(): pl.pallas_call(pack_kernel, in_specs=[pl.BlockSpec(memory_space=pl.ANY)]...  2.1 us
    ppermute x2, starting transfers between devices, swap(): return lax.ppermute(x, 'harm', [(0, 1), (1, 0)])  1.61 us
    pallas_call x2, Pallas kernels, place(): pl.pallas_call(place_kernel, in_specs=[VM] * len(args), out_specs=pl.Bloc...  1.59 us
  transfers between devices with their start and end apart: 2, of which 2 were waited for; matrix products, arithmetic and copies ran while one was open for 0% of the time, Pallas kernels for 7%

profile of v6, /device:TPU:1, one launch (start us, length us, event | category | flops | bytes accessed | tf_op | source)
XLA Modules:
  0.0 64.7 jit_solution(10916731066762503891)
XLA Ops:
  0.6 2.1 %pack.1 = (f32[2304,128]{1,0:T(8,128)S(1)}, bf16[384,128]{1,0:T(8,128)(2,1)S(1)}) custom-call(f32[1,3,32,1024]{3,2,1,0:T(8,128)} %disp.1, f32[1,3,32,1024]{3,2,1,0:T(8,128)} %direction.1, s32[1,128,1024]{2,1,0:T(8,128)} %stick.1, f32[1,4,1024]{2,1,0:T(4,128)} %refs_0_.1, f32[32,128]{1,0:T(8,128)} %refs_1_.1, f32[32,128]{1,0:T(8,128)} %refs_2_.1, ...), custom_call_target="tpu_custom_call" | custom-call | tf_op jit(solution)/shard_map/pack/pallas_call | solution.py:137
  2.7 0.0 copy-start.1
  2.8 0.0 copy-start.2
  2.8 0.0 copy-start.3
  2.8 0.0 copy-start.4
  2.8 49.5 %all_to_all.5 = f32[256,1,1152]{2,1,0:T(1,128)S(1)} all-to-all(f32[256,1,1152]{2,1,0:T(1,128)S(1)} %bitcast.10), channel_id=1, replica_groups=mesh['sector'=128,'harm'=2] {'sector','harm'}, dimensions={0} | all-to-all | bytes 2359296 | tf_op jit(solution)/shard_map/all_to_all | solution.py:303
  52.3 0.0 copy-done.1
  52.3 0.0 copy-done.2
  52.3 0.0 copy-done.3
  52.3 0.0 copy-done.4
  52.3 1.2 %send0.1 = f32[384,128]{1,0:T(8,128)S(1)} custom-call(f32[2304,128]{1,0:T(8,128)S(1)} %bitcast.7, bf16[384,256]{1,0:T(8,128)(2,1)S(1)} %copy-done.1, bf16[384,128]{1,0:T(8,128)(2,1)S(1)} %get-tuple-element.13.pull_hat, bf16[2,128,192]{2,1,0:T(8,128)(2,1)S(1)} %copy-done.2, bf16[2,64,384]{2,1,0:T(8,128)(2,1)S(1)} %copy-done.4, bf16[384,128]{1,0:T(8,128)(2,1)S(1)} %copy-done.3), custom_call_target="tpu_custom_call" | custom-call | flops 1000000000 | bytes 2000000 | tf_op jit(solution)/shard_map/send0/pallas_call | solution.py:240
  53.5 0.1 collective-permute-start
  53.6 1.6 %send1.1 = f32[384,128]{1,0:T(8,128)S(1)} custom-call(f32[2304,128]{1,0:T(8,128)S(1)} %bitcast.8, bf16[384,256]{1,0:T(8,128)(2,1)S(1)} %copy-done.1, bf16[384,128]{1,0:T(8,128)(2,1)S(1)} %get-tuple-element.13.pull_hat, bf16[2,128,192]{2,1,0:T(8,128)(2,1)S(1)} %copy-done.2, bf16[2,64,384]{2,1,0:T(8,128)(2,1)S(1)} %copy-done.4, bf16[384,128]{1,0:T(8,128)(2,1)S(1)} %copy-done.3), custom_call_target="tpu_custom_call" | custom-call | flops 1000000000 | bytes 2000000 | tf_op jit(solution)/shard_map/send1/pallas_call | solution.py:240
  55.1 0.0 copy-start
  55.2 1.5 %collective-permute-start.1 = (f32[384,128]{1,0:T(8,128)S(1)}, f32[384,128]{1,0:T(8,128)S(1)}, u32[]{:S(2)}, u32[]{:S(2)}) collective-permute-start(f32[384,128]{1,0:T(8,128)S(1)} %send1.1), channel_id=1, source_target_pairs={{0,1},{1,0},{2,3},{3,2},{4,5},{5,4},{6,7},{7,6},{8,9},{9,8},{10,11... | collective-permute-start | bytes 589832 | tf_op jit(solution)/shard_map/ppermute | solution.py:291
  56.7 1.9 %keep.1 = (f32[384,128]{1,0:T(8,128)S(1)}, f32[384,128]{1,0:T(8,128)S(1)}) custom-call(f32[2304,128]{1,0:T(8,128)S(1)} %bitcast.9, bf16[384,256]{1,0:T(8,128)(2,1)S(1)} %copy-done.1, bf16[384,128]{1,0:T(8,128)(2,1)S(1)} %get-tuple-element.13.pull_hat, bf16[2,128,192]{2,1,0:T(8,128)(2,1)S(1)} %copy-done.2, bf16[2,64,384]{2,1,0:T(8,128)(2,1)S(1)} %copy-done.4, ...), custom_call_target="tpu_custom_call" | custom-call | flops 2000000000 | bytes 2000000 | tf_op jit(solution)/shard_map/keep/pallas_call | solution.py:240
  58.6 1.1 %collective-permute-done.recv = f32[384,128]{1,0:T(8,128)S(1)} collective-permute-done((f32[384,128]{1,0:T(8,128)S(1)}, f32[384,128]{1,0:T(8,128)S(1)}, u32[]{:S(2)}, u32[]{:S(2)}) %collective-permute-start) | collective-permute-done | bytes 196640 | tf_op jit(solution)/shard_map/ppermute | solution.py:291
  59.7 0.0 copy-done
  59.7 0.8 %place0.1 = f32[768,128]{1,0:T(8,128)} custom-call(f32[384,128]{1,0:T(8,128)S(1)} %get-tuple-element.17.mine, f32[384,128]{1,0:T(8,128)S(1)} %collective-permute-done.recv, f32[768,128]{1,0:T(8,128)S(1)} %bitcast.11), custom_call_target="tpu_custom_call" | custom-call | flops 1000000 | bytes 2000000 | tf_op jit(solution)/shard_map/place0/pallas_call | solution.py:278
  60.5 3.4 %collective-permute-done.1.recv = f32[384,128]{1,0:T(8,128)S(1)} collective-permute-done((f32[384,128]{1,0:T(8,128)S(1)}, f32[384,128]{1,0:T(8,128)S(1)}, u32[]{:S(2)}, u32[]{:S(2)}) %collective-permute-start.1) | collective-permute-done | bytes 196640 | tf_op jit(solution)/shard_map/ppermute | solution.py:291
  63.9 0.8 %place1.1 = f32[768,128]{1,0:T(8,128)} custom-call(f32[384,128]{1,0:T(8,128)S(1)} %get-tuple-element.20.mine, f32[384,128]{1,0:T(8,128)S(1)} %collective-permute-done.1.recv), custom_call_target="tpu_custom_call" | custom-call | flops 1000000 | bytes 2000000 | tf_op jit(solution)/shard_map/place1/pallas_call | solution.py:278
Async XLA Ops:
  2.7 49.6 %copy-start.1 = (bf16[384,256]{1,0:T(8,128)(2,1)S(1)}, bf16[384,256]{1,0:T(8,128)(2,1)}, u32[]{:S(2)}) copy-start(bf16[384,256]{1,0:T(8,128)(2,1)} %constant.11.clone.pair) | copy-start | bytes 589828
  2.8 49.5 %copy-start.2 = (bf16[2,128,192]{2,1,0:T(8,128)(2,1)S(1)}, bf16[2,128,192]{2,1,0:T(8,128)(2,1)}, u32[]{:S(2)}) copy-start(bf16[2,128,192]{2,1,0:T(8,128)(2,1)} %constant.12.clone.to_time) | copy-start | bytes 294916
  2.8 49.5 %copy-start.3 = (bf16[384,128]{1,0:T(8,128)(2,1)S(1)}, bf16[384,128]{1,0:T(8,128)(2,1)}, u32[]{:S(2)}) copy-start(bf16[384,128]{1,0:T(8,128)(2,1)} %constant.14.clone.diff) | copy-start | bytes 294916
  2.8 49.5 %copy-start.4 = (bf16[2,64,384]{2,1,0:T(8,128)(2,1)S(1)}, bf16[2,64,384]{2,1,0:T(8,128)(2,1)}, u32[]{:S(2)}) copy-start(bf16[2,64,384]{2,1,0:T(8,128)(2,1)} %constant.13.clone.to_coef) | copy-start | bytes 294916
  53.5 6.2 %collective-permute-start = (f32[384,128]{1,0:T(8,128)S(1)}, f32[384,128]{1,0:T(8,128)S(1)}, u32[]{:S(2)}, u32[]{:S(2)}) collective-permute-start(f32[384,128]{1,0:T(8,128)S(1)} %send0.1), channel_id=1, source_target_pairs={{0,1},{1,0},{2,3},{3,2},{4,5},{5,4},{6,7},{7,6},{8,9},{9,8},{10,11... | collective-permute-start | bytes 589832 | tf_op jit(solution)/shard_map/ppermute | solution.py:291
  55.1 4.5 %copy-start = (f32[3,32,8,128]{3,2,1,0:T(8,128)S(1)}, f32[3,32,8,128]{3,2,1,0:T(8,128)}, u32[]{:S(2)}) copy-start(f32[3,32,8,128]{3,2,1,0:T(8,128)} %param.22) | copy-start | bytes 1179652
  55.2 8.7 %collective-permute-start.1 = (f32[384,128]{1,0:T(8,128)S(1)}, f32[384,128]{1,0:T(8,128)S(1)}, u32[]{:S(2)}, u32[]{:S(2)}) collective-permute-start(f32[384,128]{1,0:T(8,128)S(1)} %send1.1), channel_id=1, source_target_pairs={{0,1},{1,0},{2,3},{3,2},{4,5},{5,4},{6,7},{7,6},{8,9},{9,8},{10,11... | collective-permute-start | bytes 589832 | tf_op jit(solution)/shard_map/ppermute | solution.py:291

commit v7 on v6

--- a/solution.py
+++ b/solution.py
@@ -34,7 +34,7 @@
     hart_diff = hart - np.roll(hart, -1, axis=0)
     to_time, to_coef = [], []
     for h in range(2):
-        own = np.roll(np.roll(basis, -32 * h, axis=0), -64 * h, axis=1)
+        own = np.roll(basis, -32 * h, axis=0)
         hi, lo = split_np(own.T)
         to_time.append(np.concatenate([hi, hi, lo], 1))
         hi, lo = split_np(own * (2.0 / N))
@@ -119,7 +119,10 @@
         e = ve[:, :, cols].reshape(96, N)
         z = vz[:, cols].astype(F32)
         scr0[k] = jnp.concatenate([d, e[:32]], 0).T
-        scr1[k] = jnp.concatenate([e[32:], z], 0).T
+        mixed = jnp.where(
+            h == 0, jnp.concatenate([z, e[32:]], 0), jnp.concatenate([e[32:], z], 0)
+        )
+        scr1[k] = mixed.T
         base = 32 * ROWS * k
         for i in range(4):
             to = pl.ds(base + 2 * i, 32, stride=ROWS)
@@ -180,17 +183,21 @@
     n0, kn, kt, mu = tall
     states = [[[], [], []], [[], [], []]]
     stick = []
+    lane = lax.broadcasted_iota(jnp.int32, (N, N), 1)
     for i in range(4):
-        parts = []
-        for half in (h, 1 - h):
-            left = got[pl.ds(half * ROWS + 2 * i, N, stride=step), :].T
-            right = got[pl.ds(half * ROWS + 2 * i + 1, N, stride=step), :].T
-            parts.append((left, right))
-        for q in range(3 + 3 * max(fields)):
-            side, at = (0, q) if q < 4 else (1, q - 4)
-            coefs = [p[side][HALF * at : HALF * at + HALF] for p in parts]
-            states[q // 3][q % 3].append(coefs)
-        stick.append(jnp.concatenate([p[1][64:128] for p in parts], 0))
+        lefts = [got[pl.ds(b * ROWS + 2 * i, N, stride=step), :].T for b in (h, 1 - h)]
+        rights = [got[pl.ds(b * ROWS + 2 * i + 1, N, stride=step), :] for b in range(2)]
+        stick.append(jnp.where(lane < 64, rights[0], rights[1]).T)
+        for ch in range(3):
+            states[0][ch].append([p[HALF * ch : HALF * ch + HALF] for p in lefts])
+        if max(fields):
+            states[1][0].append([p[96:128] for p in lefts])
+            moved = jnp.where(lane < 64, rights[1], rights[0]).T
+            low, high = moved[0:64], moved[64:128]
+            both = [jnp.where(h == 0, high, low), jnp.where(h == 0, low, high)]
+            for ch in (1, 2):
+                rows = slice(HALF * (ch - 1), HALF * ch)
+                states[1][ch].append([p[rows] for p in both])
     stick = jnp.concatenate(stick, 1)
     wave = to_time[h]
 

time: 64.8 us -> 64.8 us (level)
  no operation moved by 1% of the time
where the time goes in v7:
time: 64.8 us; the launch traced here: 64.6 us
  blocking collectives  49.5 us (76%)
  Pallas kernels  8.27 us (13%)
  waiting for transfers between devices  4.51 us (7%)
  starting transfers between devices  1.62 us (2%)
  between operations  0.72 us (1%)
    all_to_all x1, blocking collectives, body(): lax.all_to_all(packed.reshape(256, 1, ROWS * N), ('sector', 'harm'), 0, 0...  49.5 us
    pallas_call x3, Pallas kernels, contact(): pl.pallas_call(functools.partial(contact_kernel, fields, part), in_specs=...  4.57 us
    ppermute x2, waiting for transfers between devices, swap(): return lax.ppermute(x, 'harm', [(0, 1), (1, 0)])  4.51 us
    pallas_call x1, Pallas kernels, pack(): pl.pallas_call(pack_kernel, in_specs=[pl.BlockSpec(memory_space=pl.ANY)]...  2.11 us
    ppermute x2, starting transfers between devices, swap(): return lax.ppermute(x, 'harm', [(0, 1), (1, 0)])  1.62 us
    pallas_call x2, Pallas kernels, place(): pl.pallas_call(place_kernel, in_specs=[VM] * len(args), out_specs=pl.Bloc...  1.59 us
  transfers between devices with their start and end apart: 2, of which 2 were waited for; matrix products, arithmetic and copies ran while one was open for 0% of the time, Pallas kernels for 7%

profile of v7, /device:TPU:1, one launch (start us, length us, event | category | flops | bytes accessed | tf_op | source)
XLA Modules:
  0.0 64.6 jit_solution(3200015750785570242)
XLA Ops:
  0.6 2.1 %pack.1 = (f32[2304,128]{1,0:T(8,128)S(1)}, bf16[384,128]{1,0:T(8,128)(2,1)S(1)}) custom-call(f32[1,3,32,1024]{3,2,1,0:T(8,128)} %disp.1, f32[1,3,32,1024]{3,2,1,0:T(8,128)} %direction.1, s32[1,128,1024]{2,1,0:T(8,128)} %stick.1, f32[1,4,1024]{2,1,0:T(4,128)} %refs_0_.1, f32[32,128]{1,0:T(8,128)} %refs_1_.1, f32[32,128]{1,0:T(8,128)} %refs_2_.1, ...), custom_call_target="tpu_custom_call" | custom-call | tf_op jit(solution)/shard_map/pack/pallas_call | solution.py:140
  2.7 0.0 copy-start.1
  2.8 0.0 copy-start.2
  2.8 0.0 copy-start.3
  2.8 0.0 copy-start.4
  2.8 49.5 %all_to_all.5 = f32[256,1,1152]{2,1,0:T(1,128)S(1)} all-to-all(f32[256,1,1152]{2,1,0:T(1,128)S(1)} %bitcast.10), channel_id=1, replica_groups=mesh['sector'=128,'harm'=2] {'sector','harm'}, dimensions={0} | all-to-all | bytes 2359296 | tf_op jit(solution)/shard_map/all_to_all | solution.py:310
  52.3 0.0 copy-done.1
  52.3 0.0 copy-done.2
  52.3 0.0 copy-done.3
  52.3 0.0 copy-done.4
  52.3 1.2 %send0.1 = f32[384,128]{1,0:T(8,128)S(1)} custom-call(f32[2304,128]{1,0:T(8,128)S(1)} %bitcast.7, bf16[384,256]{1,0:T(8,128)(2,1)S(1)} %copy-done.1, bf16[384,128]{1,0:T(8,128)(2,1)S(1)} %get-tuple-element.13.pull_hat, bf16[2,128,192]{2,1,0:T(8,128)(2,1)S(1)} %copy-done.2, bf16[2,64,384]{2,1,0:T(8,128)(2,1)S(1)} %copy-done.4, bf16[384,128]{1,0:T(8,128)(2,1)S(1)} %copy-done.3), custom_call_target="tpu_custom_call" | custom-call | flops 1000000000 | bytes 2000000 | tf_op jit(solution)/shard_map/send0/pallas_call | solution.py:247
  53.5 0.1 collective-permute-start
  53.6 1.5 %send1.1 = f32[384,128]{1,0:T(8,128)S(1)} custom-call(f32[2304,128]{1,0:T(8,128)S(1)} %bitcast.8, bf16[384,256]{1,0:T(8,128)(2,1)S(1)} %copy-done.1, bf16[384,128]{1,0:T(8,128)(2,1)S(1)} %get-tuple-element.13.pull_hat, bf16[2,128,192]{2,1,0:T(8,128)(2,1)S(1)} %copy-done.2, bf16[2,64,384]{2,1,0:T(8,128)(2,1)S(1)} %copy-done.4, bf16[384,128]{1,0:T(8,128)(2,1)S(1)} %copy-done.3), custom_call_target="tpu_custom_call" | custom-call | flops 1000000000 | bytes 2000000 | tf_op jit(solution)/shard_map/send1/pallas_call | solution.py:247
  55.1 0.0 copy-start
  55.1 1.5 %collective-permute-start.1 = (f32[384,128]{1,0:T(8,128)S(1)}, f32[384,128]{1,0:T(8,128)S(1)}, u32[]{:S(2)}, u32[]{:S(2)}) collective-permute-start(f32[384,128]{1,0:T(8,128)S(1)} %send1.1), channel_id=1, source_target_pairs={{0,1},{1,0},{2,3},{3,2},{4,5},{5,4},{6,7},{7,6},{8,9},{9,8},{10,11... | collective-permute-start | bytes 589832 | tf_op jit(solution)/shard_map/ppermute | solution.py:298
  56.6 1.9 %keep.1 = (f32[384,128]{1,0:T(8,128)S(1)}, f32[384,128]{1,0:T(8,128)S(1)}) custom-call(f32[2304,128]{1,0:T(8,128)S(1)} %bitcast.9, bf16[384,256]{1,0:T(8,128)(2,1)S(1)} %copy-done.1, bf16[384,128]{1,0:T(8,128)(2,1)S(1)} %get-tuple-element.13.pull_hat, bf16[2,128,192]{2,1,0:T(8,128)(2,1)S(1)} %copy-done.2, bf16[2,64,384]{2,1,0:T(8,128)(2,1)S(1)} %copy-done.4, ...), custom_call_target="tpu_custom_call" | custom-call | flops 2000000000 | bytes 2000000 | tf_op jit(solution)/shard_map/keep/pallas_call | solution.py:247
  58.5 1.1 %collective-permute-done.recv = f32[384,128]{1,0:T(8,128)S(1)} collective-permute-done((f32[384,128]{1,0:T(8,128)S(1)}, f32[384,128]{1,0:T(8,128)S(1)}, u32[]{:S(2)}, u32[]{:S(2)}) %collective-permute-start) | collective-permute-done | bytes 196640 | tf_op jit(solution)/shard_map/ppermute | solution.py:298
  59.6 0.0 copy-done
  59.6 0.8 %place0.1 = f32[768,128]{1,0:T(8,128)} custom-call(f32[384,128]{1,0:T(8,128)S(1)} %get-tuple-element.17.mine, f32[384,128]{1,0:T(8,128)S(1)} %collective-permute-done.recv, f32[768,128]{1,0:T(8,128)S(1)} %bitcast.11), custom_call_target="tpu_custom_call" | custom-call | flops 1000000 | bytes 2000000 | tf_op jit(solution)/shard_map/place0/pallas_call | solution.py:285
  60.5 3.4 %collective-permute-done.1.recv = f32[384,128]{1,0:T(8,128)S(1)} collective-permute-done((f32[384,128]{1,0:T(8,128)S(1)}, f32[384,128]{1,0:T(8,128)S(1)}, u32[]{:S(2)}, u32[]{:S(2)}) %collective-permute-start.1) | collective-permute-done | bytes 196640 | tf_op jit(solution)/shard_map/ppermute | solution.py:298
  63.9 0.8 %place1.1 = f32[768,128]{1,0:T(8,128)} custom-call(f32[384,128]{1,0:T(8,128)S(1)} %get-tuple-element.20.mine, f32[384,128]{1,0:T(8,128)S(1)} %collective-permute-done.1.recv), custom_call_target="tpu_custom_call" | custom-call | flops 1000000 | bytes 2000000 | tf_op jit(solution)/shard_map/place1/pallas_call | solution.py:285
Async XLA Ops:
  2.7 49.6 %copy-start.1 = (bf16[384,256]{1,0:T(8,128)(2,1)S(1)}, bf16[384,256]{1,0:T(8,128)(2,1)}, u32[]{:S(2)}) copy-start(bf16[384,256]{1,0:T(8,128)(2,1)} %constant.11.clone.pair) | copy-start | bytes 589828
  2.8 49.5 %copy-start.2 = (bf16[2,128,192]{2,1,0:T(8,128)(2,1)S(1)}, bf16[2,128,192]{2,1,0:T(8,128)(2,1)}, u32[]{:S(2)}) copy-start(bf16[2,128,192]{2,1,0:T(8,128)(2,1)} %constant.12.clone.to_time) | copy-start | bytes 294916
  2.8 49.5 %copy-start.3 = (bf16[384,128]{1,0:T(8,128)(2,1)S(1)}, bf16[384,128]{1,0:T(8,128)(2,1)}, u32[]{:S(2)}) copy-start(bf16[384,128]{1,0:T(8,128)(2,1)} %constant.14.clone.diff) | copy-start | bytes 294916
  2.8 49.5 %copy-start.4 = (bf16[2,64,384]{2,1,0:T(8,128)(2,1)S(1)}, bf16[2,64,384]{2,1,0:T(8,128)(2,1)}, u32[]{:S(2)}) copy-start(bf16[2,64,384]{2,1,0:T(8,128)(2,1)} %constant.13.clone.to_coef) | copy-start | bytes 294916
  53.5 6.2 %collective-permute-start = (f32[384,128]{1,0:T(8,128)S(1)}, f32[384,128]{1,0:T(8,128)S(1)}, u32[]{:S(2)}, u32[]{:S(2)}) collective-permute-start(f32[384,128]{1,0:T(8,128)S(1)} %send0.1), channel_id=1, source_target_pairs={{0,1},{1,0},{2,3},{3,2},{4,5},{5,4},{6,7},{7,6},{8,9},{9,8},{10,11... | collective-permute-start | bytes 589832 | tf_op jit(solution)/shard_map/ppermute | solution.py:298
  55.1 4.6 %copy-start = (f32[3,32,8,128]{3,2,1,0:T(8,128)S(1)}, f32[3,32,8,128]{3,2,1,0:T(8,128)}, u32[]{:S(2)}) copy-start(f32[3,32,8,128]{3,2,1,0:T(8,128)} %param.22) | copy-start | bytes 1179652
  55.1 8.8 %collective-permute-start.1 = (f32[384,128]{1,0:T(8,128)S(1)}, f32[384,128]{1,0:T(8,128)S(1)}, u32[]{:S(2)}, u32[]{:S(2)}) collective-permute-start(f32[384,128]{1,0:T(8,128)S(1)} %send1.1), channel_id=1, source_target_pairs={{0,1},{1,0},{2,3},{3,2},{4,5},{5,4},{6,7},{7,6},{8,9},{9,8},{10,11... | collective-permute-start | bytes 589832 | tf_op jit(solution)/shard_map/ppermute | solution.py:298

commit v8 on v6

--- a/solution.py
+++ b/solution.py
@@ -84,11 +84,10 @@
     first = [
         pltpu.make_async_copy(small_hbm[k], small[k], small_sem.at[k]) for k in range(6)
     ]
-    copies = []
+    copies = [pltpu.make_async_copy(stick.at[0, samples], vz, sem.at[6])]
     for ch in range(3):
         copies.append(pltpu.make_async_copy(disp.at[0, ch], vd.at[ch], sem.at[ch]))
         copies.append(pltpu.make_async_copy(direction.at[0, ch], ve.at[ch], sem.at[3 + ch]))
-    copies.append(pltpu.make_async_copy(stick.at[0, samples], vz, sem.at[6]))
     for copy in first + copies:
         copy.start()
     for copy in first:

time: 64.8 us -> 64.9 us (level)
  no operation moved by 1% of the time
where the time goes in v8:
time: 64.9 us; the launch traced here: 64.6 us
  blocking collectives  49.5 us (76%)
  Pallas kernels  8.32 us (13%)
  waiting for transfers between devices  4.46 us (7%)
  starting transfers between devices  1.62 us (2%)
  between operations  0.72 us (1%)
    all_to_all x1, blocking collectives, body(): lax.all_to_all(packed.reshape(256, 1, ROWS * N), ('sector', 'harm'), 0, 0...  49.5 us
    pallas_call x3, Pallas kernels, contact(): pl.pallas_call(functools.partial(contact_kernel, fields, part), in_specs=...  4.62 us
    ppermute x2, waiting for transfers between devices, swap(): return lax.ppermute(x, 'harm', [(0, 1), (1, 0)])  4.46 us
    pallas_call x1, Pallas kernels, pack(): pl.pallas_call(pack_kernel, in_specs=[pl.BlockSpec(memory_space=pl.ANY)]...  2.1 us
    ppermute x2, starting transfers between devices, swap(): return lax.ppermute(x, 'harm', [(0, 1), (1, 0)])  1.62 us
    pallas_call x2, Pallas kernels, place(): pl.pallas_call(place_kernel, in_specs=[VM] * len(args), out_specs=pl.Bloc...  1.59 us
  transfers between devices with their start and end apart: 2, of which 2 were waited for; matrix products, arithmetic and copies ran while one was open for 0% of the time, Pallas kernels for 7%

profile of v8, /device:TPU:1, one launch (start us, length us, event | category | flops | bytes accessed | tf_op | source)
XLA Modules:
  0.0 64.6 jit_solution(8292763416215924993)
XLA Ops:
  0.6 2.1 %pack.1 = (f32[2304,128]{1,0:T(8,128)S(1)}, bf16[384,128]{1,0:T(8,128)(2,1)S(1)}) custom-call(f32[1,3,32,1024]{3,2,1,0:T(8,128)} %disp.1, f32[1,3,32,1024]{3,2,1,0:T(8,128)} %direction.1, s32[1,128,1024]{2,1,0:T(8,128)} %stick.1, f32[1,4,1024]{2,1,0:T(4,128)} %refs_0_.1, f32[32,128]{1,0:T(8,128)} %refs_1_.1, f32[32,128]{1,0:T(8,128)} %refs_2_.1, ...), custom_call_target="tpu_custom_call" | custom-call | tf_op jit(solution)/shard_map/pack/pallas_call | solution.py:136
  2.7 0.0 copy-start.1
  2.8 0.0 copy-start.2
  2.8 0.0 copy-start.3
  2.8 0.0 copy-start.4
  2.8 49.5 %all_to_all.5 = f32[256,1,1152]{2,1,0:T(1,128)S(1)} all-to-all(f32[256,1,1152]{2,1,0:T(1,128)S(1)} %bitcast.10), channel_id=1, replica_groups=mesh['sector'=128,'harm'=2] {'sector','harm'}, dimensions={0} | all-to-all | bytes 2359296 | tf_op jit(solution)/shard_map/all_to_all | solution.py:302
  52.3 0.0 copy-done.1
  52.3 0.0 copy-done.2
  52.3 0.0 copy-done.3
  52.3 0.0 copy-done.4
  52.3 1.2 %send0.1 = f32[384,128]{1,0:T(8,128)S(1)} custom-call(f32[2304,128]{1,0:T(8,128)S(1)} %bitcast.7, bf16[384,256]{1,0:T(8,128)(2,1)S(1)} %copy-done.1, bf16[384,128]{1,0:T(8,128)(2,1)S(1)} %get-tuple-element.13.pull_hat, bf16[2,128,192]{2,1,0:T(8,128)(2,1)S(1)} %copy-done.2, bf16[2,64,384]{2,1,0:T(8,128)(2,1)S(1)} %copy-done.4, bf16[384,128]{1,0:T(8,128)(2,1)S(1)} %copy-done.3), custom_call_target="tpu_custom_call" | custom-call | flops 1000000000 | bytes 2000000 | tf_op jit(solution)/shard_map/send0/pallas_call | solution.py:239
  53.5 0.1 collective-permute-start
  53.6 1.5 %send1.1 = f32[384,128]{1,0:T(8,128)S(1)} custom-call(f32[2304,128]{1,0:T(8,128)S(1)} %bitcast.8, bf16[384,256]{1,0:T(8,128)(2,1)S(1)} %copy-done.1, bf16[384,128]{1,0:T(8,128)(2,1)S(1)} %get-tuple-element.13.pull_hat, bf16[2,128,192]{2,1,0:T(8,128)(2,1)S(1)} %copy-done.2, bf16[2,64,384]{2,1,0:T(8,128)(2,1)S(1)} %copy-done.4, bf16[384,128]{1,0:T(8,128)(2,1)S(1)} %copy-done.3), custom_call_target="tpu_custom_call" | custom-call | flops 1000000000 | bytes 2000000 | tf_op jit(solution)/shard_map/send1/pallas_call | solution.py:239
  55.1 0.0 copy-start
  55.1 1.5 %collective-permute-start.1 = (f32[384,128]{1,0:T(8,128)S(1)}, f32[384,128]{1,0:T(8,128)S(1)}, u32[]{:S(2)}, u32[]{:S(2)}) collective-permute-start(f32[384,128]{1,0:T(8,128)S(1)} %send1.1), channel_id=1, source_target_pairs={{0,1},{1,0},{2,3},{3,2},{4,5},{5,4},{6,7},{7,6},{8,9},{9,8},{10,11... | collective-permute-start | bytes 589832 | tf_op jit(solution)/shard_map/ppermute | solution.py:290
  56.7 1.9 %keep.1 = (f32[384,128]{1,0:T(8,128)S(1)}, f32[384,128]{1,0:T(8,128)S(1)}) custom-call(f32[2304,128]{1,0:T(8,128)S(1)} %bitcast.9, bf16[384,256]{1,0:T(8,128)(2,1)S(1)} %copy-done.1, bf16[384,128]{1,0:T(8,128)(2,1)S(1)} %get-tuple-element.13.pull_hat, bf16[2,128,192]{2,1,0:T(8,128)(2,1)S(1)} %copy-done.2, bf16[2,64,384]{2,1,0:T(8,128)(2,1)S(1)} %copy-done.4, ...), custom_call_target="tpu_custom_call" | custom-call | flops 2000000000 | bytes 2000000 | tf_op jit(solution)/shard_map/keep/pallas_call | solution.py:239
  58.6 1.1 %collective-permute-done.recv = f32[384,128]{1,0:T(8,128)S(1)} collective-permute-done((f32[384,128]{1,0:T(8,128)S(1)}, f32[384,128]{1,0:T(8,128)S(1)}, u32[]{:S(2)}, u32[]{:S(2)}) %collective-permute-start) | collective-permute-done | bytes 196640 | tf_op jit(solution)/shard_map/ppermute | solution.py:290
  59.6 0.0 copy-done
  59.6 0.8 %place0.1 = f32[768,128]{1,0:T(8,128)} custom-call(f32[384,128]{1,0:T(8,128)S(1)} %get-tuple-element.17.mine, f32[384,128]{1,0:T(8,128)S(1)} %collective-permute-done.recv, f32[768,128]{1,0:T(8,128)S(1)} %bitcast.11), custom_call_target="tpu_custom_call" | custom-call | flops 1000000 | bytes 2000000 | tf_op jit(solution)/shard_map/place0/pallas_call | solution.py:277
  60.5 3.4 %collective-permute-done.1.recv = f32[384,128]{1,0:T(8,128)S(1)} collective-permute-done((f32[384,128]{1,0:T(8,128)S(1)}, f32[384,128]{1,0:T(8,128)S(1)}, u32[]{:S(2)}, u32[]{:S(2)}) %collective-permute-start.1) | collective-permute-done | bytes 196640 | tf_op jit(solution)/shard_map/ppermute | solution.py:290
  63.9 0.8 %place1.1 = f32[768,128]{1,0:T(8,128)} custom-call(f32[384,128]{1,0:T(8,128)S(1)} %get-tuple-element.20.mine, f32[384,128]{1,0:T(8,128)S(1)} %collective-permute-done.1.recv), custom_call_target="tpu_custom_call" | custom-call | flops 1000000 | bytes 2000000 | tf_op jit(solution)/shard_map/place1/pallas_call | solution.py:277
Async XLA Ops:
  2.7 49.6 %copy-start.1 = (bf16[384,256]{1,0:T(8,128)(2,1)S(1)}, bf16[384,256]{1,0:T(8,128)(2,1)}, u32[]{:S(2)}) copy-start(bf16[384,256]{1,0:T(8,128)(2,1)} %constant.11.clone.pair) | copy-start | bytes 589828
  2.8 49.5 %copy-start.2 = (bf16[2,128,192]{2,1,0:T(8,128)(2,1)S(1)}, bf16[2,128,192]{2,1,0:T(8,128)(2,1)}, u32[]{:S(2)}) copy-start(bf16[2,128,192]{2,1,0:T(8,128)(2,1)} %constant.12.clone.to_time) | copy-start | bytes 294916
  2.8 49.5 %copy-start.3 = (bf16[384,128]{1,0:T(8,128)(2,1)S(1)}, bf16[384,128]{1,0:T(8,128)(2,1)}, u32[]{:S(2)}) copy-start(bf16[384,128]{1,0:T(8,128)(2,1)} %constant.14.clone.diff) | copy-start | bytes 294916
  2.8 49.5 %copy-start.4 = (bf16[2,64,384]{2,1,0:T(8,128)(2,1)S(1)}, bf16[2,64,384]{2,1,0:T(8,128)(2,1)}, u32[]{:S(2)}) copy-start(bf16[2,64,384]{2,1,0:T(8,128)(2,1)} %constant.13.clone.to_coef) | copy-start | bytes 294916
  53.5 6.2 %collective-permute-start = (f32[384,128]{1,0:T(8,128)S(1)}, f32[384,128]{1,0:T(8,128)S(1)}, u32[]{:S(2)}, u32[]{:S(2)}) collective-permute-start(f32[384,128]{1,0:T(8,128)S(1)} %send0.1), channel_id=1, source_target_pairs={{0,1},{1,0},{2,3},{3,2},{4,5},{5,4},{6,7},{7,6},{8,9},{9,8},{10,11... | collective-permute-start | bytes 589832 | tf_op jit(solution)/shard_map/ppermute | solution.py:290
  55.1 4.5 %copy-start = (f32[3,32,8,128]{3,2,1,0:T(8,128)S(1)}, f32[3,32,8,128]{3,2,1,0:T(8,128)}, u32[]{:S(2)}) copy-start(f32[3,32,8,128]{3,2,1,0:T(8,128)} %param.22) | copy-start | bytes 1179652
  55.1 8.7 %collective-permute-start.1 = (f32[384,128]{1,0:T(8,128)S(1)}, f32[384,128]{1,0:T(8,128)S(1)}, u32[]{:S(2)}, u32[]{:S(2)}) collective-permute-start(f32[384,128]{1,0:T(8,128)S(1)} %send1.1), channel_id=1, source_target_pairs={{0,1},{1,0},{2,3},{3,2},{4,5},{5,4},{6,7},{7,6},{8,9},{9,8},{10,11... | collective-permute-start | bytes 589832 | tf_op jit(solution)/shard_map/ppermute | solution.py:290
